TPU v7x, 256 devices: a whole 4x4x8 slice. The times are simulated.
256 devices in a mesh: view: 32 (over y, x, core), strip: 8 (over z).
Axes of the slice: x: 4, y: 4, z: 8, core: 2. Of those that a mesh axis runs over, the one named last changes fastest.
Arguments:
- tokens: bfloat16 [32, 1024, 1536], P('view', 'strip'), may hold values from -48 to 48
- source_ids: int32 [32, 8, 5], replicated, may hold values from 0 to 255, as said below
- source_count: int32 [32, 8], replicated, may hold values from 2 to 5, as said below
- self_query: bfloat16 [1536, 1536], P(None, 'strip'), may hold values from -24 to 24
- self_key: bfloat16 [1536, 1536], P(None, 'strip'), may hold values from -24 to 24
- self_value: bfloat16 [1536, 1536], P(None, 'strip'), may hold values from -0.15625 to 0.15625
- self_out: bfloat16 [1536, 1536], P('strip'), may hold values from -1.1953125 to 1.1953125
- cross_query: bfloat16 [1536, 1536], P(None, 'strip'), may hold values from -24 to 24
- cross_key: bfloat16 [1536, 1536], P(None, 'strip'), may hold values from -24 to 24
- cross_value: bfloat16 [1536, 1536], P(None, 'strip'), may hold values from -0.15625 to 0.15625
- cross_out: bfloat16 [1536, 1536], P('strip'), may hold values from -1.1953125 to 1.1953125
- mlp_up: bfloat16 [1536, 6144], P(None, 'strip'), may hold values from -0.15625 to 0.15625
- mlp_down: bfloat16 [6144, 1536], P('strip'), may hold values from -0.078125 to 0.078125
Outputs:
- mixed: bfloat16 [32, 1024, 1536], P('view', 'strip')
Inputs may be any that keep to these rules, and one draw needn't show every extreme that they name: `source_ids`: entry k of strip s of view v names a strip of another view than v; entries with k >= source_count[v, s] are unused. Among all 40 entries of one destination view, used or not, each other view is named at most 2 times, and some view exactly 2 times. `source_count`: every view has a strip with all 5 entries in use.
All inputs are finite; a program needn't handle non-finite values.
Results may differ from a plain program's by a relative error of at most 0.015.
Values may be sent and summed in bfloat16 or wider, within the bound.
No kernel may reach another device: no remote copies, remote signals or barrier semaphores. Data moves between devices by JAX's collectives and lax.ppermute only.
A program may use at most 128 MiB of HBM per device.

v0:
```python
import math

import jax
import jax.numpy as jnp
from jax import lax
from jax.sharding import PartitionSpec as P

HEAD_DIM = 64
SLOTS = 5


def rms_rows(values_in):
    widened = values_in.astype(jnp.float32)
    scaled = widened * lax.rsqrt(jnp.mean(widened * widened, axis=-1, keepdims=True) + 1e-06)
    return scaled.astype(jnp.bfloat16)


def attend_heads(query_heads, key_heads, value_heads, key_mask):
    scale = 1.0 / math.sqrt(HEAD_DIM)
    scores = (
        jnp.einsum("qhe,khe->hqk", query_heads, key_heads, preferred_element_type=jnp.float32)
        * scale
    )
    scores = jnp.where(key_mask[None, None, :], scores, -1e30)
    weights = jax.nn.softmax(scores, axis=-1).astype(jnp.bfloat16)
    mixed_heads = jnp.einsum(
        "hqk,khe->qhe", weights, value_heads, preferred_element_type=jnp.float32
    )
    return mixed_heads.reshape(mixed_heads.shape[0], -1).astype(jnp.bfloat16)


def branch_term(mixed_rows, weight):
    return jnp.dot(mixed_rows, weight, preferred_element_type=jnp.float32)


def per_device(
    tokens,
    source_ids,
    source_count,
    self_query,
    self_key,
    self_value,
    self_out,
    cross_query,
    cross_key,
    cross_value,
    cross_out,
    mlp_up,
    mlp_down,
):
    n_view = lax.axis_size("view")
    n_strip = lax.axis_size("strip")
    my_view = lax.axis_index("view")
    strip_rows = tokens.shape[1]
    head_cols = self_query.shape[1]
    heads_here = head_cols // HEAD_DIM
    capacity = (n_strip * SLOTS + n_view - 2) // (n_view - 1)
    normed = rms_rows(tokens[0])
    stacked = jnp.concatenate(
        [self_query, self_key, self_value, cross_query, cross_key, cross_value, mlp_up], 1
    )
    split_at = 6 * head_cols
    product = jnp.dot(
        lax.all_gather(normed, "strip", axis=0, tiled=True),
        stacked,
        preferred_element_type=jnp.float32,
    )
    projected = jnp.concatenate(
        [product[:, :split_at], jax.nn.gelu(product[:, split_at:])], 1
    ).astype(jnp.bfloat16)
    total_rows = projected.shape[0]
    flat_ids = source_ids.reshape(n_view, -1)
    source_view = flat_ids // n_strip
    source_strip = flat_ids % n_strip
    entry_count = flat_ids.shape[1]
    entry_order = jnp.arange(entry_count, dtype=jnp.int32)
    earlier = entry_order[None, :] < entry_order[:, None]
    same_view = source_view[:, :, None] == source_view[:, None, :]
    slot_rank = jnp.sum(jnp.logical_and(same_view, earlier[None]), axis=2)
    slot_index = jnp.arange(capacity, dtype=jnp.int32)
    slot_match = jnp.logical_and(
        (source_view == my_view)[:, :, None], slot_rank[:, :, None] == slot_index[None, None, :]
    )
    strip_table = jnp.sum(jnp.where(slot_match, source_strip[:, :, None], 0), axis=1)
    cross_pairs = projected[:, 4 * head_cols : 6 * head_cols].reshape(
        n_strip, strip_rows, 2 * head_cols
    )
    outgoing = cross_pairs[strip_table]
    received = lax.all_to_all(outgoing, "view", split_axis=0, concat_axis=0, tiled=True)

    def head_block(column_block):
        return projected[:, column_block * head_cols : (column_block + 1) * head_cols].reshape(
            total_rows, heads_here, HEAD_DIM
        )

    self_mix = attend_heads(
        head_block(0), head_block(1), head_block(2), jnp.ones((total_rows,), dtype=bool)
    )
    hidden = projected[:, split_at:]
    my_source = lax.dynamic_index_in_dim(source_view, my_view, 0, keepdims=False)
    my_rank = lax.dynamic_index_in_dim(slot_rank, my_view, 0, keepdims=False)
    picked = received.reshape(n_view * capacity, strip_rows, 2 * head_cols)[
        my_source * capacity + my_rank
    ]
    picked = picked.reshape(n_strip, SLOTS * strip_rows, 2 * head_cols)
    my_count = lax.dynamic_index_in_dim(source_count, my_view, 0, keepdims=False)
    key_valid = jnp.repeat(
        jnp.arange(SLOTS, dtype=jnp.int32)[None, :] < my_count[:, None], strip_rows, axis=1
    )
    cross_heads = projected[:, 3 * head_cols : 4 * head_cols].reshape(
        n_strip, strip_rows, heads_here, HEAD_DIM
    )
    picked_keys = picked[:, :, :head_cols].reshape(
        n_strip, SLOTS * strip_rows, heads_here, HEAD_DIM
    )
    picked_values = picked[:, :, head_cols:].reshape(
        n_strip, SLOTS * strip_rows, heads_here, HEAD_DIM
    )
    cross_mix = jax.vmap(attend_heads)(cross_heads, picked_keys, picked_values, key_valid).reshape(
        total_rows, head_cols
    )
    early_part = lax.psum_scatter(
        (branch_term(self_mix, self_out) + branch_term(hidden, mlp_down)).astype(jnp.bfloat16),
        "strip",
        scatter_dimension=0,
        tiled=True,
    ).astype(jnp.float32)
    cross_part = lax.psum_scatter(
        branch_term(cross_mix, cross_out).astype(jnp.bfloat16),
        "strip",
        scatter_dimension=0,
        tiled=True,
    ).astype(jnp.float32)
    summed = early_part + cross_part
    return (tokens[0].astype(jnp.float32) + summed).astype(jnp.bfloat16)[None]


def solution(mesh):
    in_specs = (
        P("view", "strip", None),
        P(),
        P(),
        P(None, "strip"),
        P(None, "strip"),
        P(None, "strip"),
        P("strip", None),
        P(None, "strip"),
        P(None, "strip"),
        P(None, "strip"),
        P("strip", None),
        P(None, "strip"),
        P("strip", None),
    )
    out_specs = P("view", "strip", None)
    return jax.shard_map(
        per_device, mesh=mesh, in_specs=in_specs, out_specs=out_specs, check_vma=False
    )
```

profile of v0, /device:TPU:12, one launch (start us, length us, event | category | flops | bytes accessed | tf_op | source)
XLA Modules:
  0.0 247.6 jit_solution(7047850341351948367)
XLA Ops:
  13.5 2.2 copy.71
  15.7 2.2 copy.72
  17.9 2.2 copy.73
  20.2 2.2 copy.74
  22.4 2.2 copy.75
  24.6 10.7 %concatenate.5 = bf16[1536,1920]{1,0:T(8,128)(2,1)} concatenate(bf16[1536,192]{1,0:T(8,128)(2,1)S(1)} %copy.70, bf16[1536,192]{1,0:T(8,128)(2,1)} %copy.71, bf16[1536,192]{1,0:T(8,128)(2,1)} %copy.72, bf16[1536,192]{1,0:T(8,128)(2,1)} %copy.73, bf16[1536,192]{1,0:T(8,128)(2,1)} %copy.74, bf16[1536,192]{1,0:T(8,128)(2,1)} %copy.75, bf16[1536,768]{1,0:T(8,128)(2,1)} %param.24), dimensions={1} | concatenate | bytes 11796480 | tf_op jit(solution)/shard_map/concatenate | solution.py:59
  35.9 21.9 %all-gather.2.cloned.1.call-done = bf16[1024,1536]{1,0:T(8,128)(2,1)} async-done(((bf16[128,1536]{1,0:T(8,128)(2,1)}), bf16[1024,1536]{1,0:T(8,128)(2,1)}) %all-gather.2.cloned.1.call-update) | async-done | bytes 3145744 | tf_op jit(solution)/shard_map/all_gather | solution.py:64
  57.7 11.9 %fusion.61 = (bf16[1024,1920]{1,0:T(8,128)(2,1)S(1)}, f32[1024,1920]{1,0:T(8,128)}) fusion(bf16[1024,1536]{1,0:T(8,128)(2,1)} %all-gather.2.cloned.1.call-done, bf16[1536,1920]{1,0:T(8,128)(2,1)} %concatenate.5), kind=kOutput, calls=%fused_computation.87 | convolution fusion | flops 6041763840 | bytes 20840448 | tf_op jit(solution)/shard_map/dot_general | solution.py:63
  74.8 4.1 %gather_fusion = bf16[64,128,384]{2,1,0:T(8,128)(2,1)} fusion(bf16[8,128,384]{2,1,0:T(8,128)(2,1)S(1)} %bitcast.59, s32[1024]{0:T(1024)} %pad_clamp_fusion.1), kind=kCustom, calls=%fused_computation | custom fusion | bytes 12583168 | tf_op jit(solution)/shard_map/gather | solution.py:88
  79.0 7.4 %all-to-all-start = ((bf16[32,2,128,384]{3,2,1,0:T(8,128)(2,1)}), bf16[32,2,128,384]{3,2,1,0:T(8,128)(2,1)}, u32[]{:S(2)}, u32[]{:S(2)}) async-start(bf16[32,2,128,384]{3,2,1,0:T(8,128)(2,1)} %bitcast.60), calls=%async_computation.1 | async-start | bytes 12582912 | tf_op jit(solution)/shard_map/all_to_all | solution.py:89
  86.7 7.7 %fusion.22 = f32[1024,1536]{1,0:T(8,128)} fusion(bf16[768,1536]{1,0:T(8,128)(2,1)S(1)} %copy-done, f32[1024,1920]{1,0:T(8,128)} %get-tuple-element.14), kind=kOutput, calls=%fused_computation.30 | convolution fusion | flops 2422996992 | bytes 11796480 | tf_op jit(solution)/shard_map/dot_general | solution.py:33
  94.4 7.4 %fusion.67 = (f32[3,1024]{1,0:T(4,128)S(1)}, f32[3,1024,1024]{1,2,0:T(8,128)}) fusion(bf16[1024,3,64]{0,2,1:T(8,128)(2,1)S(1)} %bitcast.68, bf16[1024,3,64]{0,2,1:T(8,128)(2,1)S(1)} %bitcast.67), kind=kOutput, calls=%fused_computation.89 | convolution fusion | flops 412091392 | bytes 13381632 | tf_op jit(solution)/shard_map/sub | solution.py:25
  101.9 5.8 %fusion.29 = bf16[3,64,1024]{2,1,0:T(8,128)(2,1)S(1)} fusion(bf16[1024,3,64]{0,2,1:T(8,128)(2,1)S(1)} %bitcast.69, f32[3,1024,1024]{1,2,0:T(8,128)} %get-tuple-element.18, f32[3,1024]{1,0:T(4,128)S(1)} %get-tuple-element.17), kind=kOutput, calls=%fused_computation.36 | convolution fusion | flops 409141248 | bytes 13381632 | tf_op jit(solution)/shard_map/hqk,khe->qhe/dot_general | solution.py:26
  107.8 5.6 %add_convert_fusion = bf16[1024,1536]{1,0:T(8,128)(2,1)} fusion(f32[1024,1536]{1,0:T(8,128)} %fusion.22, bf16[1024,192]{0,1:T(8,128)(2,1)S(1)} %bitcast.66, bf16[192,1536]{1,0:T(8,128)(2,1)S(1)} %copy-done.5), kind=kOutput, calls=%fused_computation.11 | convolution fusion | flops 607125504 | bytes 10420224 | tf_op jit(solution)/shard_map/dot_general | solution.py:33
  115.0 44.2 %all-to-all-done = bf16[32,2,128,384]{3,2,1,0:T(8,128)(2,1)} async-done(((bf16[32,2,128,384]{3,2,1,0:T(8,128)(2,1)}), bf16[32,2,128,384]{3,2,1,0:T(8,128)(2,1)}, u32[]{:S(2)}, u32[]{:S(2)}) %all-to-all-start) | async-done | bytes 6291488 | tf_op jit(solution)/shard_map/all_to_all | solution.py:89
  159.2 6.1 %gather_fusion.1 = bf16[40,128,384]{2,1,0:T(8,128)(2,1)} fusion(bf16[64,128,384]{2,1,0:T(8,128)(2,1)} %bitcast.10, s32[1024]{0:T(1024)S(1)} %pad_clamp_fusion), kind=kCustom, calls=%fused_computation.1 | custom fusion | bytes 7864480 | tf_op jit(solution)/shard_map/gather | solution.py:102
  165.3 6.4 %fusion.60 = (bf16[8,640,192]{2,1,0:T(8,128)(2,1)}, bf16[8,640,192]{2,1,0:T(8,128)(2,1)}) fusion(bf16[8,640,384]{2,1,0:T(8,128)(2,1)} %bitcast.61), kind=kLoop, calls=%fused_computation.86 | loop fusion | bytes 7864320 | tf_op jit(solution)/shard_map/slice | solution.py:113
  171.6 3.0 %copy.88 = bf16[8,640,192]{1,2,0:T(8,128)(2,1)S(1)} copy(bf16[8,640,192]{2,1,0:T(8,128)(2,1)} %get-tuple-element.11) | data formatting | bytes 3932160 | tf_op jit(solution)/shard_map/slice | solution.py:113
  174.7 4.3 %copy.86 = bf16[8,640,192]{1,2,0:T(8,128)(2,1)} copy(bf16[8,640,192]{2,1,0:T(8,128)(2,1)} %get-tuple-element.12) | data formatting | bytes 3932160 | tf_op jit(solution)/shard_map/slice | solution.py:116
  179.0 4.8 %fusion.62 = (f32[8,3,128]{2,1,0:T(4,128)S(1)}, f32[8,3,128,640]{3,2,1,0:T(8,128)}) fusion(pred[8,640]{1,0:T(8,128)(4,1)S(1)} %broadcast_bitcast_fusion, bf16[8,640,3,64]{1,3,2,0:T(8,128)(2,1)S(1)} %bitcast.63, bf16[8,128,3,64]{1,0,3,2:T(8,128)(2,1)S(1)} %bitcast.70), kind=kOutput, calls=%fused_computation.88 | convolution fusion | flops 259523200 | bytes 10241024 | tf_op jit(solution)/shard_map/vmap()/sub | solution.py:25
  183.8 5.6 %fusion.30 = bf16[8,128,3,64]{1,3,2,0:T(8,128)(2,1)S(1)} fusion(bf16[8,640,3,64]{1,3,2,0:T(8,128)(2,1)} %bitcast.64, f32[8,3,128,640]{3,2,1,0:T(8,128)} %get-tuple-element.16, f32[8,3,128]{2,1,0:T(4,128)S(1)} %get-tuple-element.15), kind=kOutput, calls=%fused_computation.37 | convolution fusion | flops 255787008 | bytes 10235904 | tf_op jit(solution)/shard_map/vmap(hqk,khe->qhe)/dot_general | solution.py:26
  189.7 2.7 %convolution_convert_fusion = bf16[1024,1536]{1,0:T(8,128)(2,1)} fusion(bf16[192,1536]{1,0:T(8,128)(2,1)S(1)} %copy-done.6, bf16[24,8,8,128]{3,2,1,0:T(8,128)(2,1)S(1)} %bitcast.62), kind=kOutput, calls=%fused_computation.21 | convolution fusion | flops 605552640 | bytes 4128768 | tf_op jit(solution)/shard_map/dot_general | solution.py:33
  192.4 46.6 %reduce-scatter.5.cloned.1.call-done = bf16[128,1536]{1,0:T(8,128)(2,1)} async-done(((bf16[1024,1536]{1,0:T(8,128)(2,1)}), bf16[128,1536]{1,0:T(8,128)(2,1)}) %reduce-scatter.5.cloned.1.call-update) | async-done | bytes 393232 | tf_op jit(solution)/shard_map/reduce_scatter | solution.py:128
  239.0 2.0 fusion.36
  (56 shorter events, 14.9 us)
Async XLA Ops:
  6.5 80.1 %copy-start = (bf16[768,1536]{1,0:T(8,128)(2,1)S(1)}, bf16[768,1536]{1,0:T(8,128)(2,1)}, u32[]{:S(2)}) copy-start(bf16[768,1536]{1,0:T(8,128)(2,1)} %param.25) | copy-start | bytes 7077892
  6.5 51.2 %all-gather.2.cloned.1.call-start = ((), (), s32[]{:S(2)}) async-start(), calls=%async_computation.3 | async-start | bytes 3538944 | tf_op jit(solution)/shard_map/all_gather | solution.py:64
  11.4 0.6 copy-start.8
  79.0 80.2 %all-to-all-start = ((bf16[32,2,128,384]{3,2,1,0:T(8,128)(2,1)}), bf16[32,2,128,384]{3,2,1,0:T(8,128)(2,1)}, u32[]{:S(2)}, u32[]{:S(2)}) async-start(bf16[32,2,128,384]{3,2,1,0:T(8,128)(2,1)} %bitcast.60), calls=%async_computation.1 | async-start | bytes 12582912 | tf_op jit(solution)/shard_map/all_to_all | solution.py:89
  86.4 106.0 %reduce-scatter.3.cloned.1.call-start = ((), (), s32[]{:S(2)}) async-start(), calls=%async_computation.4 | async-start | bytes 3538944 | tf_op jit(solution)/shard_map/reduce_scatter | solution.py:122
  86.7 7.7 %copy-start.7 = (bf16[1024,192]{0,1:T(8,128)(2,1)S(1)}, bf16[1024,192]{0,1:T(8,128)(2,1)}, u32[]{:S(2)}) copy-start(bf16[1024,192]{0,1:T(8,128)(2,1)} %copy.77) | copy-start | bytes 1179652
  94.4 7.4 %copy-start.4 = (bf16[1024,192]{1,0:T(8,128)(2,1)S(1)}, bf16[1024,192]{1,0:T(8,128)(2,1)}, u32[]{:S(2)}) copy-start(bf16[1024,192]{1,0:T(8,128)(2,1)} %get-tuple-element.10) | copy-start | bytes 1179652
  101.9 5.9 %copy-start.5 = (bf16[192,1536]{1,0:T(8,128)(2,1)S(1)}, bf16[192,1536]{1,0:T(8,128)(2,1)}, u32[]{:S(2)}) copy-start(bf16[192,1536]{1,0:T(8,128)(2,1)} %param.19) | copy-start | bytes 1769476
  107.8 5.9 %copy-start.9 = (s32[32,8]{0,1:T(8,128)S(1)}, s32[32,8]{0,1:T(8,128)}, u32[]{:S(2)}) copy-start(s32[32,8]{0,1:T(8,128)} %param.15) | copy-start | bytes 3076
  107.8 6.9 %copy-start.3 = (bf16[1024,192]{1,0:T(8,128)(2,1)S(1)}, bf16[1024,192]{1,0:T(8,128)(2,1)}, u32[]{:S(2)}) copy-start(bf16[1024,192]{1,0:T(8,128)(2,1)} %get-tuple-element.8) | copy-start | bytes 1179652
  113.4 125.6 %reduce-scatter.5.cloned.1.call-start = ((), (), s32[]{:S(2)}) async-start(), calls=%async_computation.5 | async-start | bytes 3538944 | tf_op jit(solution)/shard_map/reduce_scatter | solution.py:128
  183.8 5.9 %copy-start.6 = (bf16[192,1536]{1,0:T(8,128)(2,1)S(1)}, bf16[192,1536]{1,0:T(8,128)(2,1)}, u32[]{:S(2)}) copy-start(bf16[192,1536]{1,0:T(8,128)(2,1)} %param.23) | copy-start | bytes 1769476
  189.7 49.4 %copy-start.2 = (bf16[1,128,1536]{2,1,0:T(8,128)(2,1)S(1)}, bf16[1,128,1536]{2,1,0:T(8,128)(2,1)}, u32[]{:S(2)}) copy-start(bf16[1,128,1536]{2,1,0:T(8,128)(2,1)} %param.13) | copy-start | bytes 1179652
  189.7 51.4 %copy-start.1 = (bf16[768,1536]{1,0:T(8,128)(2,1)S(1)}, bf16[768,1536]{1,0:T(8,128)(2,1)}, u32[]{:S(2)}) copy-start(bf16[768,1536]{1,0:T(8,128)(2,1)} %param.25) | copy-start | bytes 7077892
Sparse Core Ops, SparseCore 0:
  9.9 47.8 all-gather.1
  113.6 45.5 reduce-scatter.2
  192.5 46.4 reduce-scatter.4
where the time goes:
time: 249 us; the launch traced here: 248 us
  waiting for transfers between devices  113 us (45%)
  local copies, waits for them, and re-layouts  54.6 us (22%)
  matrix products  51.5 us (21%)
  between operations  13.3 us (5%)
  starting transfers between devices  7.93 us (3%)
  other arithmetic  7.46 us (3%)
    reduce_scatter x1, waiting for transfers between devices, per_device(): lax.psum_scatter(branch_term(cross_mix, cross_out).astype(jnp.bfloat16),...  46.6 us
    all_to_all x1, waiting for transfers between devices, per_device(): lax.all_to_all(outgoing, 'view', split_axis=0, concat_axis=0, tiled=True)  44.2 us
    all_gather x1, waiting for transfers between devices, per_device(): lax.all_gather(normed, 'strip', axis=0, tiled=True)  21.9 us
    dot_general x3, matrix products, branch_term(): return jnp.dot(mixed_rows, weight, preferred_element_type=jnp.float32)  16 us
    unnamed x28, local copies, waits for them, and re-layouts  13.7 us
    sub x2, matrix products, attend_heads(): weights = jax.nn.softmax(scores, axis=-1).astype(jnp.bfloat16)  12.1 us
    dot_general x1, matrix products, per_device(): jnp.dot(lax.all_gather(normed, 'strip', axis=0, tiled=True), stacked, pre...  11.9 us
    dot_general x2, matrix products, attend_heads(): jnp.einsum('hqk,khe->qhe', weights, value_heads, preferred_element_type=j...  11.4 us
  transfers between devices with their start and end apart: 4, of which 3 were waited for; matrix products, arithmetic and copies ran while one was open for 35% of the time, Pallas kernels for 0%

commit v1 on v0

v1 whole, which is shorter than its diff:
```python
import math

import jax
import jax.numpy as jnp
from jax import lax
from jax.experimental import pallas as pl
from jax.experimental.pallas import tpu as pltpu
from jax.sharding import PartitionSpec as P


HEAD_DIM = 64
SLOTS = 5
GROUP = 2 * HEAD_DIM
SCALE_LOG2 = math.log2(math.e) / math.sqrt(HEAD_DIM)
BF16 = jnp.bfloat16
F32 = jnp.float32


def rms_rows(values_in):
    widened = values_in.astype(F32)
    scaled = widened * lax.rsqrt(jnp.mean(widened * widened, axis=-1, keepdims=True) + 1e-06)
    return scaled.astype(BF16)


def ring_pairs(size, step):
    return [(i, (i + step) % size) for i in range(size)]


def shift(value, size, step):
    return lax.ppermute(value, "strip", ring_pairs(size, step))


def pair_heads(keys, values):
    pieces = []
    for at in range(0, keys.shape[1], HEAD_DIM):
        pieces += [keys[:, at : at + HEAD_DIM], values[:, at : at + HEAD_DIM]]
    return jnp.concatenate(pieces, 1).astype(BF16)


def pad_heads(queries):
    return pair_heads(queries, jnp.zeros_like(queries))


def dot(a, b):
    return jnp.dot(a, b, preferred_element_type=F32)


def dot_rows(a, b):
    return lax.dot_general(a, b, (((1,), (1,)), ((), ())), preferred_element_type=F32)


def slot_of(strip):
    paired = jnp.where(strip < 4, 2 * strip - 1, 2 * (7 - strip))
    return jnp.where(strip == 0, 6, jnp.where(strip == 4, 7, paired))


OFFSETS = (7, 1, 6, 2, 5, 3, 0, 4)


def whole(array):
    return pl.BlockSpec(array.shape, lambda *_: (0,) * array.ndim)


def project_rows(x, weights, outs):
    sq, sk, sv, cq, up, ck, cv = weights
    self_q, self_kv, cross_q, hidden = outs[:4]
    if ck is not None:
        outs[4][0] = pair_heads(dot_rows(x, ck[...]), dot_rows(x, cv[...]))
    self_kv[0] = pair_heads(dot_rows(x, sk[...]), dot_rows(x, sv[...]))
    self_q[0] = pad_heads(dot_rows(x, sq[...]))
    cross_q[0] = pad_heads(dot_rows(x, cq[...]))
    hidden[0] = jax.nn.gelu(dot(x, up[...])).astype(BF16)


def project(blocks, weights, held, place, with_cross):
    sq, sk, sv, cq, up, ck, cv = weights
    operands = [*blocks, sq, sk, sv, cq, up] + ([ck, cv] if with_cross else [])
    count = len(blocks)
    rows = sum(block.shape[0] for block in blocks)
    cols, ff = sq.shape[0], up.shape[1]
    widths = [2 * cols, 2 * cols, 2 * cols, ff] + ([2 * cols] if with_cross else [])
    n_held = 0 if held is None else len(held)

    def kernel(*refs):
        x = jnp.concatenate([ref[...] for ref in refs[:count]], 0)
        inputs = list(refs[count : len(operands)])
        if not with_cross:
            inputs += [None, None]
        project_rows(x, inputs, refs[len(operands) + n_held :])

    depth = 4
    return pl.pallas_call(
        kernel,
        grid=(1,),
        in_specs=[whole(a) for a in operands] + [pl.BlockSpec(memory_space=pl.ANY)] * n_held,
        out_specs=[pl.BlockSpec((1, rows, n), lambda i: (place, 0, 0)) for n in widths],
        out_shape=[jax.ShapeDtypeStruct((depth, rows, n), BF16) for n in widths],
        input_output_aliases={len(operands) + i: i for i in range(n_held)},
        name="project",
    )(*operands, *([] if held is None else held))


def pack_items(table, blocks, paired, ck, cv, capacity):
    count = len(blocks)
    depth, both, width = paired.shape
    rows = both // 2
    items = table.shape[0]
    n_view = items // capacity
    steps = 4
    block = n_view // steps

    def kernel(table_ref, *refs):
        xs, (pair_ref, ck_ref, cv_ref, out_ref, held) = refs[:count], refs[count:]
        step = pl.program_id(0)

        @pl.when(step == 0)
        def _():
            x = jnp.concatenate([ref[...] for ref in xs], 0)
            last = pair_heads(dot_rows(x, ck_ref[...]), dot_rows(x, cv_ref[...]))
            held[2 * depth - 2] = last[:rows]
            held[2 * depth - 1] = last[rows:]
            for k in range(depth - 1):
                held[2 * k] = pair_ref[k, :rows]
                held[2 * k + 1] = pair_ref[k, rows:]

        for i in range(block):
            for j in range(capacity):
                out_ref[i, j] = held[table_ref[j * n_view + step * block + i]]

    return pl.pallas_call(
        kernel,
        grid_spec=pltpu.PrefetchScalarGridSpec(
            num_scalar_prefetch=1,
            grid=(steps,),
            in_specs=[whole(x) for x in blocks]
            + [pl.BlockSpec((depth - 1, both, width), lambda i, t: (0, 0, 0)), whole(ck), whole(cv)],
            out_specs=pl.BlockSpec((block, capacity, rows, width), lambda i, t: (i, 0, 0, 0)),
            scratch_shapes=[pltpu.VMEM((2 * depth, rows, width), BF16)],
        ),
        out_shape=jax.ShapeDtypeStruct((n_view, capacity, rows, width), BF16),
        name="pack_items",
    )(table, *blocks, paired, ck, cv)


def early_kernel(q_ref, kv_ref, hidden_ref, out_w, down_w, result):
    mixes = []
    for at in range(0, q_ref.shape[2], GROUP):
        pairs = kv_ref[:, at : at + GROUP]
        scores = dot_rows(q_ref[0, :, at : at + GROUP], pairs)
        top = jnp.max(scores, axis=1, keepdims=True)
        weights = jnp.exp2((scores - top) * SCALE_LOG2)
        total = jnp.sum(weights, axis=1, keepdims=True)
        mix = dot(weights.astype(BF16), pairs)
        mixes.append(mix[:, HEAD_DIM:] / total)
    mix = jnp.concatenate(mixes, 1).astype(BF16)
    result[0] = (dot(mix, out_w[...]) + dot(hidden_ref[0], down_w[...])).astype(BF16)


def early_terms(q, kv, hidden, out_w, down_w, first, count):
    depth, rows, width = q.shape
    kv = kv.reshape(depth * rows, width)
    ff, cols = hidden.shape[2], out_w.shape[1]
    return pl.pallas_call(
        early_kernel,
        grid=(count,),
        in_specs=[
            pl.BlockSpec((1, rows, width), lambda i: (first + i, 0, 0)),
            whole(kv),
            pl.BlockSpec((1, rows, ff), lambda i: (first + i, 0, 0)),
            whole(out_w),
            whole(down_w),
        ],
        out_specs=pl.BlockSpec((1, rows, cols), lambda i: (i, 0, 0)),
        out_shape=jax.ShapeDtypeStruct((count, rows, cols), BF16),
        name="early_terms",
    )(q, kv, hidden, out_w, down_w)


def add_pair(ahead, behind, terms, at):
    rows = terms.shape[1] // 2

    def kernel(ahead_ref, behind_ref, term_ref, ahead_out, behind_out):
        def add(received, term):
            return (received.astype(F32) + term.astype(F32)).astype(BF16)

        if ahead.shape[0] < rows:
            n = ahead.shape[0]
            ahead_out[:n] = add(ahead_ref[...], term_ref[0, rows : rows + n])
            ahead_out[n:] = term_ref[0, rows + n :]
            behind_out[:n] = term_ref[0, :n]
            behind_out[n:] = add(behind_ref[...], term_ref[0, n:rows])
        else:
            ahead_out[...] = add(ahead_ref[...], term_ref[0, rows:])
            behind_out[...] = add(behind_ref[...], term_ref[0, :rows])

    shape = jax.ShapeDtypeStruct((rows, terms.shape[2]), BF16)
    return pl.pallas_call(
        kernel,
        grid=(1,),
        in_specs=[whole(ahead), whole(behind), pl.BlockSpec((1, *terms.shape[1:]), lambda i: (at, 0, 0))],
        out_specs=[pl.BlockSpec(shape.shape, lambda i: (0, 0))] * 2,
        out_shape=[shape, shape],
        name="add_pair",
    )(ahead, behind, terms)


def cross_attention(items, counts, me, q, received, strips):
    rows, width = received.shape[1:]
    heads = width // GROUP

    def kernel(item_ref, count_ref, me_ref, q_ref, received_ref, out_ref, held, sems):
        def strip_at(place):
            offset = OFFSETS[0]
            for k in range(1, strips):
                offset = jnp.where(place == k, OFFSETS[k], offset)
            return lax.rem(me_ref[0] + offset, strips)

        def copies(place):
            strip = strip_at(place)
            return [
                pltpu.make_async_copy(
                    received_ref.at[item_ref[k * strips + strip]],
                    held.at[place, pl.ds(k * rows, rows)],
                    sems.at[place, k],
                )
                for k in range(SLOTS)
            ]

        @pl.loop(0, strips)
        def _(place):
            for copy in copies(place):
                copy.start()

        @pl.loop(0, strips)
        def _(place):
            for copy in copies(place):
                copy.wait()
            strip = strip_at(place)
            in_use = lax.broadcasted_iota(jnp.int32, (SLOTS * rows, rows), 0) < count_ref[strip] * rows
            queries = q_ref[place // 2, pl.ds(lax.rem(place, 2) * rows, rows), :]
            for head in range(heads):
                at = head * GROUP
                pairs = held[place, :, at : at + GROUP]
                scores = dot_rows(pairs, queries[:, at : at + GROUP])
                scores = jnp.where(in_use, scores, -1e30)
                top = jnp.max(scores, axis=0, keepdims=True)
                weights = jnp.exp2((scores - top) * SCALE_LOG2)
                total = jnp.sum(weights, axis=0, keepdims=True)
                mix = lax.dot_general(
                    pairs, weights.astype(BF16), (((0,), (0,)), ((), ())), preferred_element_type=F32
                )
                out_ref[strip, head * HEAD_DIM : (head + 1) * HEAD_DIM] = (
                    mix[HEAD_DIM:] / total
                ).astype(BF16)

    smem = pl.BlockSpec(memory_space=pltpu.SMEM)
    return pl.pallas_call(
        kernel,
        in_specs=[smem, smem, smem, pl.BlockSpec(memory_space=pltpu.VMEM), pl.BlockSpec(memory_space=pl.ANY)],
        out_specs=pl.BlockSpec(memory_space=pltpu.VMEM),
        out_shape=jax.ShapeDtypeStruct((strips, width // 2, rows), BF16),
        scratch_shapes=[
            pltpu.VMEM((strips, SLOTS * rows, width), BF16),
            pltpu.SemaphoreType.DMA((strips, SLOTS)),
        ],
        name="cross_attention",
    )(items, counts, me, q, received)


def collect(pieces, far):
    strips = len(pieces) + 1
    rows, cols = pieces[0].shape
    blocks = pieces[: strips // 2] + list(far) + pieces[strips // 2 :]

    def kernel(*refs):
        out_ref, at = refs[-1], 0
        for ref in refs[:-1]:
            n = ref.shape[0]
            out_ref[at // rows, at % rows : at % rows + n] = ref[...]
            at += n

    vmem = pl.BlockSpec(memory_space=pltpu.VMEM)
    return pl.pallas_call(
        kernel,
        in_specs=[vmem] * len(blocks),
        out_specs=vmem,
        out_shape=jax.ShapeDtypeStruct((strips, rows, cols), BF16),
        name="collect",
    )(*blocks)


def finish(place, mix, mine, other, token_rows, ahead, behind, terms, at):
    strips, width, half = mine.shape
    rows = token_rows.shape[0]
    cols = 256

    def kernel(place_ref, mix_ref, mine_ref, other_ref, token_ref, ahead_ref, behind_ref, own_ref, out_ref):
        me, side = place_ref[0], place_ref[1]
        step = pl.program_id(0)
        for weights, part in ((mine_ref, side), (other_ref, 1 - side)):
            total = 0.0
            for j in range(strips):
                total = total + lax.dot_general(
                    mix_ref[lax.rem(me + j, strips)],
                    weights[j],
                    (((0,), (0,)), ((), ())),
                    preferred_element_type=F32,
                )
            here = pl.ds(pl.multiple_of(part * half + step * cols, 128), cols)
            early = ahead_ref[:, here].astype(F32) + behind_ref[:, here].astype(F32)
            early = early + own_ref[0, :, here].astype(F32)
            out_ref[:, here] = (token_ref[:, here].astype(F32) + (total + early)).astype(BF16)

    return pl.pallas_call(
        kernel,
        grid_spec=pltpu.PrefetchScalarGridSpec(
            num_scalar_prefetch=1,
            grid=(half // cols,),
            in_specs=[
                whole(mix),
                pl.BlockSpec((strips, width, cols), lambda i, p: (0, 0, i)),
                pl.BlockSpec((strips, width, cols), lambda i, p: (0, 0, i)),
                whole(token_rows),
                whole(ahead),
                whole(behind),
                pl.BlockSpec((1, rows, terms.shape[2]), lambda i, p: (at, 0, 0)),
            ],
            out_specs=whole(token_rows),
        ),
        out_shape=jax.ShapeDtypeStruct(token_rows.shape, BF16),
        name="finish",
    )(place, mix, mine, other, token_rows, ahead, behind, terms)


def routing(source_ids, source_count, my_view, my_strip, n_view, n_strip):
    lists = source_ids.transpose(2, 1, 0).reshape(-1, n_view)
    order = lax.broadcasted_iota(jnp.int32, lists.shape, 0)
    keyed = order * n_strip + lists % n_strip
    match = lists // n_strip == my_view
    first = jnp.min(jnp.where(match, keyed, lists.size * n_strip), axis=0)
    last = jnp.max(jnp.where(match, keyed, -1), axis=0)
    strips = jnp.stack([first, jnp.maximum(last, 0)]) % n_strip
    table = slot_of((strips - my_strip + n_strip) % n_strip)
    mine = lax.dynamic_slice_in_dim(lists, my_view, 1, 1) // n_strip
    count = mine.shape[0]
    earlier = lax.broadcasted_iota(jnp.int32, (count, count), 0) < lax.broadcasted_iota(
        jnp.int32, (count, count), 1
    )
    again = jnp.max(jnp.where(jnp.logical_and(mine == mine.T, earlier), 1, 0), axis=0)
    items = mine[:, 0] * 2 + again
    counts = lax.dynamic_slice_in_dim(source_count, my_view, 1, 0)[0]
    return table.reshape(-1), items, counts


def per_device(
    tokens,
    source_ids,
    source_count,
    self_query,
    self_key,
    self_value,
    self_out,
    cross_query,
    cross_key,
    cross_value,
    cross_out,
    mlp_up,
    mlp_down,
):
    n_view = lax.axis_size("view")
    n_strip = lax.axis_size("strip")
    my_view = lax.axis_index("view")
    my_strip = lax.axis_index("strip")
    side = my_view % 2
    capacity = 2
    routes = routing(source_ids, source_count, my_view, my_strip, n_view, n_strip)
    table, items, counts = lax.optimization_barrier(routes)

    weights = [self_query.T, self_key.T, self_value.T, cross_query.T, mlp_up, cross_key.T, cross_value.T]

    def both(up, down):
        return shift(up, n_strip, 1), shift(down, n_strip, -1)

    normed = rms_rows(tokens[0])
    half_rows = normed.shape[0] // 2
    ahead, behind, held = normed, normed, None
    ahead, behind = both(ahead, behind)
    for step in range(3):
        pair = [ahead, behind]
        if step < 2:
            ahead, behind = both(ahead, behind)
        else:
            ahead, behind = both(ahead[:half_rows], behind[half_rows:])
        held = project(pair, weights, held, step, True)
    blocks = [normed, ahead, behind]
    outgoing = pack_items(table, blocks, held[4], weights[5], weights[6], capacity)
    received = lax.all_to_all(outgoing, "view", split_axis=0, concat_axis=0, tiled=True)
    received = received.reshape(n_view * capacity, *outgoing.shape[2:])

    half = cross_out.shape[1] // 2
    my_half = lax.dynamic_slice_in_dim(cross_out, side * half, half, 1)
    my_half, outgoing, blocks = lax.optimization_barrier((my_half, outgoing, blocks))
    ahead, behind, found = my_half, my_half, {0: my_half}
    for step in range(1, 4):
        ahead, behind = both(ahead, behind)
        found[n_strip - step], found[step] = ahead, behind
    part = my_half.shape[0] // 2
    far = both(ahead[:part], behind[part:])
    my_halves = collect([found[j] for j in range(n_strip) if j != n_strip // 2], far)
    other_halves = lax.ppermute(my_halves, "view", [(i, i ^ 1) for i in range(n_view)])

    self_q, self_kv, cross_q, hidden = project(blocks, weights, held[:4], 3, False)
    late = early_terms(self_q, self_kv, hidden, self_out, mlp_down, 2, 2)
    soon = early_terms(self_q, self_kv, hidden, self_out, mlp_down, 0, 2)
    rows = normed.shape[0]
    ahead, behind = both(late[1, rows : rows + half_rows], late[1, rows + half_rows :])
    for terms, at in ((late, 0), (soon, 1), (soon, 0)):
        ahead, behind = add_pair(ahead, behind, terms, at)
        ahead, behind = both(ahead, behind)

    place = jnp.stack([my_strip, side]).astype(jnp.int32)
    cross_mix = cross_attention(items, counts, place[:1], cross_q, received, n_strip)
    cross_mix = lax.all_to_all(cross_mix, "strip", split_axis=0, concat_axis=0, tiled=True)
    return finish(place, cross_mix, my_halves, other_halves, tokens[0], ahead, behind, late, 1)[None]


def solution(mesh):
    in_specs = (
        P("view", "strip", None),
        P(),
        P(),
        P(None, "strip"),
        P(None, "strip"),
        P(None, "strip"),
        P("strip", None),
        P(None, "strip"),
        P(None, "strip"),
        P(None, "strip"),
        P("strip", None),
        P(None, "strip"),
        P("strip", None),
    )
    out_specs = P("view", "strip", None)

    return jax.shard_map(
        per_device, mesh=mesh, in_specs=in_specs, out_specs=out_specs, check_vma=False
    )
```

time: 249 us -> 203 us (0.82)
  Pallas kernels: 0 us -> 69.7 us
  matrix products: 51.5 us -> 0 us
  waiting for transfers between devices: 113 us -> 62.4 us
  starting transfers between devices: 7.93 us -> 54.1 us
  local copies, waits for them, and re-layouts: 54.6 us -> 10.7 us
  between operations: 13.3 us -> 0.36 us
    pallas_call x0 -> x13, Pallas kernels: none -> 69.7 us  [the longest x4 22.6 us: project(): pl.pallas_call(kernel, grid=(1,), in_specs=[whole(a) for a in operands] +...]
    ppermute x0 -> x25, waiting for transfers between devices: none -> 62.4 us  [the longest x24 62.4 us: shift(): return lax.ppermute(value, 'strip', ring_pairs(size, step))]
    reduce_scatter x2 -> x0, waiting for transfers between devices: 46.6 us -> none  [the longest x1 46.6 us: per_device(): lax.psum_scatter(branch_term(cross_mix, cross_out).astype(jnp.bfloat16),...]
    all_to_all x1, waiting for transfers between devices: 44.2 us -> 0.01 us  [per_device(): lax.all_to_all(outgoing, 'view', split_axis=0, concat_axis=0, tiled=True)]
    ppermute x0 -> x25, starting transfers between devices: none -> 42.9 us  [the longest x24 42.9 us: shift(): return lax.ppermute(value, 'strip', ring_pairs(size, step))]
    dot_general x6 -> x0, matrix products: 39.3 us -> none  [the longest x3 16 us: branch_term(): return jnp.dot(mixed_rows, weight, preferred_element_type=jnp.float32)]
    all_gather x1 -> x0, waiting for transfers between devices: 21.9 us -> none  [per_device(): lax.all_gather(normed, 'strip', axis=0, tiled=True)]
    slice x9 -> x4, local copies, waits for them, and re-layouts: 19.2 us -> 0.76 us  [the longest x2 0.74 us: per_device(): ahead, behind = both(ahead[:half_rows], behind[half_rows:])]
  transfers between devices with their start and end apart: 4 -> 27, of which waited for: 3 -> 11; matrix products, arithmetic and copies ran while one was open for 35% -> 3% of each run, Pallas kernels for 0% -> 28%
where the time goes in v1:
time: 203 us; the launch traced here: 202 us
  Pallas kernels  69.7 us (34%)
  waiting for transfers between devices  62.4 us (31%)
  starting transfers between devices  54.1 us (27%)
  local copies, waits for them, and re-layouts  10.7 us (5%)
  other arithmetic  5.12 us (3%)
    ppermute x24, waiting for transfers between devices, shift(): return lax.ppermute(value, 'strip', ring_pairs(size, step))  62.4 us
    ppermute x24, starting transfers between devices, shift(): return lax.ppermute(value, 'strip', ring_pairs(size, step))  42.9 us
    pallas_call x4, Pallas kernels, project(): pl.pallas_call(kernel, grid=(1,), in_specs=[whole(a) for a in operands] +...  22.6 us
    pallas_call x2, Pallas kernels, early_terms(): pl.pallas_call(early_kernel, grid=(count,), in_specs=[pl.BlockSpec((1, ro...  16.1 us
    pallas_call x1, Pallas kernels, cross_attention(): pl.pallas_call(kernel, in_specs=[smem, smem, smem, pl.BlockSpec(memory_sp...  8.86 us
    all_to_all x1, starting transfers between devices, per_device(): lax.all_to_all(outgoing, 'view', split_axis=0, concat_axis=0, tiled=True)  7.71 us
    pallas_call x3, Pallas kernels, add_pair(): pl.pallas_call(kernel, grid=(1,), in_specs=[whole(ahead), whole(behind),...  6.97 us
    unnamed x53, local copies, waits for them, and re-layouts  6.53 us
  transfers between devices with their start and end apart: 27, of which 11 were waited for; matrix products, arithmetic and copies ran while one was open for 3% of the time, Pallas kernels for 28%

profile of v1, /device:TPU:12, one launch (start us, length us, event | category | flops | bytes accessed | tf_op | source)
XLA Modules:
  0.0 202.3 jit_solution(6130004613706427317)
XLA Ops:
  2.4 5.9 %collective-permute-start.4 = (bf16[128,1536]{1,0:T(8,128)(2,1)S(1)}, bf16[128,1536]{1,0:T(8,128)(2,1)S(1)}, u32[]{:S(2)}, u32[]{:S(2)}) collective-permute-start(bf16[128,1536]{1,0:T(8,128)(2,1)S(1)} %fusion.1.refs_0_), channel_id=1, source_target_pairs={{0,7},{1,0},{2,1},{3,2},{4,3},{5,4},{6,5},{7,6},{8,15},{9,8},{10,9... | collective-permute-start | bytes 1179656 | tf_op jit(solution)/shard_map/ppermute | solution.py:30
  10.0 6.7 %collective-permute-done.4.refs_1_ = bf16[128,1536]{1,0:T(8,128)(2,1)S(1)} collective-permute-done((bf16[128,1536]{1,0:T(8,128)(2,1)S(1)}, bf16[128,1536]{1,0:T(8,128)(2,1)S(1)}, u32[]{:S(2)}, u32[]{:S(2)}) %collective-permute-start.4) | collective-permute-done | bytes 393248 | tf_op jit(solution)/shard_map/ppermute | solution.py:30
  16.7 3.7 %collective-permute-start.5 = (bf16[128,1536]{1,0:T(8,128)(2,1)S(1)}, bf16[128,1536]{1,0:T(8,128)(2,1)S(1)}, u32[]{:S(2)}, u32[]{:S(2)}) collective-permute-start(bf16[128,1536]{1,0:T(8,128)(2,1)S(1)} %collective-permute-done.4.refs_1_), channel_id=1, source_target_pairs={{0,7},{1,0},{2,1},{3,2},{4,3},{5,4},{6,5},{7,6},{8,15},{9,8},{10,9... | collective-permute-start | bytes 1179656 | tf_op jit(solution)/shard_map/ppermute | solution.py:30
  20.4 7.5 %collective-permute-done.5.refs_1_ = bf16[128,1536]{1,0:T(8,128)(2,1)S(1)} collective-permute-done((bf16[128,1536]{1,0:T(8,128)(2,1)S(1)}, bf16[128,1536]{1,0:T(8,128)(2,1)S(1)}, u32[]{:S(2)}, u32[]{:S(2)}) %collective-permute-start.5) | collective-permute-done | bytes 393248 | tf_op jit(solution)/shard_map/ppermute | solution.py:30
  27.9 3.7 %collective-permute-start.6 = (bf16[128,1536]{1,0:T(8,128)(2,1)S(1)}, bf16[128,1536]{1,0:T(8,128)(2,1)S(1)}, u32[]{:S(2)}, u32[]{:S(2)}) collective-permute-start(bf16[128,1536]{1,0:T(8,128)(2,1)S(1)} %collective-permute-done.5.refs_1_), channel_id=1, source_target_pairs={{0,7},{1,0},{2,1},{3,2},{4,3},{5,4},{6,5},{7,6},{8,15},{9,8},{10,9... | collective-permute-start | bytes 1179656 | tf_op jit(solution)/shard_map/ppermute | solution.py:30
  33.9 4.4 %collective-permute-done.6.refs_1_ = bf16[128,1536]{1,0:T(8,128)(2,1)S(1)} collective-permute-done((bf16[128,1536]{1,0:T(8,128)(2,1)S(1)}, bf16[128,1536]{1,0:T(8,128)(2,1)S(1)}, u32[]{:S(2)}, u32[]{:S(2)}) %collective-permute-start.6) | collective-permute-done | bytes 393248 | tf_op jit(solution)/shard_map/ppermute | solution.py:30
  38.3 3.8 %collective-permute-start.7 = (bf16[64,1536]{1,0:T(8,128)(2,1)S(1)}, bf16[64,1536]{1,0:T(8,128)(2,1)S(1)}, u32[]{:S(2)}, u32[]{:S(2)}) collective-permute-start(bf16[64,1536]{1,0:T(8,128)(2,1)S(1)} %slice.25), channel_id=1, source_target_pairs={{0,7},{1,0},{2,1},{3,2},{4,3},{5,4},{6,5},{7,6},{8,15},{9,8},{10,9... | collective-permute-start | bytes 589832 | tf_op jit(solution)/shard_map/ppermute | solution.py:30
  43.4 5.8 %project.4 = (bf16[4,256,384]{2,1,0:T(8,128)(2,1)}, bf16[4,256,384]{2,1,0:T(8,128)(2,1)}, bf16[4,256,384]{2,1,0:T(8,128)(2,1)}, bf16[4,256,768]{2,1,0:T(8,128)(2,1)}, bf16[4,256,384]{2,1,0:T(8,128)(2,1)}) custom-call(bf16[128,1536]{1,0:T(8,128)(2,1)} %copy-done.16, bf16[128,1536]{1,0:T(8,128)(2,1)} %copy-done.15, bf16[192,1536]{1,0:T(8,128)(2,1)} %bitcast.67, ...), custom_call_target="tpu_custom_call" | custom-call | tf_op jit(solution)/shard_map/project/pallas_call | solution.py:92
  49.2 5.8 %project.5 = (bf16[4,256,384]{2,1,0:T(8,128)(2,1)}, bf16[4,256,384]{2,1,0:T(8,128)(2,1)}, bf16[4,256,384]{2,1,0:T(8,128)(2,1)}, bf16[4,256,768]{2,1,0:T(8,128)(2,1)}, bf16[4,256,384]{2,1,0:T(8,128)(2,1)}) custom-call(bf16[128,1536]{1,0:T(8,128)(2,1)} %copy-done.12, ...), custom_call_target="tpu_custom_call", output_to_operand_aliasing={{0}: (9, {}), {1}: (10, {}), {2}: (11, {}), {3}: (12, {}), ... | custom-call | tf_op jit(solution)/shard_map/project/pallas_call | solution.py:92
  55.1 5.8 %project.6 = (bf16[4,256,384]{2,1,0:T(8,128)(2,1)}, bf16[4,256,384]{2,1,0:T(8,128)(2,1)}, bf16[4,256,384]{2,1,0:T(8,128)(2,1)}, bf16[4,256,768]{2,1,0:T(8,128)(2,1)}, bf16[4,256,384]{2,1,0:T(8,128)(2,1)}) custom-call(bf16[128,1536]{1,0:T(8,128)(2,1)} %copy-done.6, ...), custom_call_target="tpu_custom_call", output_to_operand_aliasing={{0}: (9, {}), {1}: (10, {}), {2}: (11, {}), {3}: (12, {}), ... | custom-call | tf_op jit(solution)/shard_map/project/pallas_call | solution.py:92
  61.6 6.3 %pack_items.1 = bf16[32,2,128,384]{3,2,1,0:T(8,128)(2,1)} custom-call(s32[64]{0:T(128)} %compare_select_fusion.6.table_ref, bf16[128,1536]{1,0:T(8,128)(2,1)} %copy-done.1, bf16[64,1536]{1,0:T(8,128)(2,1)} %copy-done.8, bf16[64,1536]{1,0:T(8,128)(2,1)} %copy-done.7, bf16[4,256,384]{2,1,0:T(8,128)(2,1)} %get-tuple-element.50.refs_3_, ...), custom_call_target="tpu_custom_call" | custom-call | tf_op jit(solution)/shard_map/pack_items/pallas_call | solution.py:130
  67.9 7.7 %all-to-all-start = ((bf16[32,2,128,384]{3,2,1,0:T(8,128)(2,1)}), bf16[32,2,128,384]{3,2,1,0:T(8,128)(2,1)}, u32[]{:S(2)}, u32[]{:S(2)}) async-start(bf16[32,2,128,384]{3,2,1,0:T(8,128)(2,1)} %pack_items.1), calls=%async_computation | async-start | bytes 12582912 | tf_op jit(solution)/shard_map/all_to_all | solution.py:397
  79.1 7.2 %collective-permute-done.11.refs_8_ = bf16[192,768]{1,0:T(8,128)(2,1)S(1)} collective-permute-done((bf16[192,768]{1,0:T(8,128)(2,1)S(1)}, bf16[192,768]{1,0:T(8,128)(2,1)S(1)}, u32[]{:S(2)}, u32[]{:S(2)}) %collective-permute-start.11) | collective-permute-done | bytes 294944 | tf_op jit(solution)/shard_map/ppermute | solution.py:30
  89.6 6.5 %collective-permute-done.12.refs_7_ = bf16[192,768]{1,0:T(8,128)(2,1)S(1)} collective-permute-done((bf16[192,768]{1,0:T(8,128)(2,1)S(1)}, bf16[192,768]{1,0:T(8,128)(2,1)S(1)}, u32[]{:S(2)}, u32[]{:S(2)}) %collective-permute-start.12) | collective-permute-done | bytes 294944 | tf_op jit(solution)/shard_map/ppermute | solution.py:30
  99.3 5.8 %collective-permute-done.13.refs_6_ = bf16[192,768]{1,0:T(8,128)(2,1)S(1)} collective-permute-done((bf16[192,768]{1,0:T(8,128)(2,1)S(1)}, bf16[192,768]{1,0:T(8,128)(2,1)S(1)}, u32[]{:S(2)}, u32[]{:S(2)}) %collective-permute-start.13) | collective-permute-done | bytes 294944 | tf_op jit(solution)/shard_map/ppermute | solution.py:30
  116.0 5.1 %project.7 = (bf16[4,256,384]{2,1,0:T(8,128)(2,1)}, bf16[4,256,384]{2,1,0:T(8,128)(2,1)}, bf16[4,256,384]{2,1,0:T(8,128)(2,1)}, bf16[4,256,768]{2,1,0:T(8,128)(2,1)}) custom-call(bf16[128,1536]{1,0:T(8,128)(2,1)} %copy-done.1, bf16[64,1536]{1,0:T(8,128)(2,1)} %copy-done.8, ...), custom_call_target="tpu_custom_call", output_to_operand_aliasing={{0}: (8, {}), {1}: (9, {}), {2}: (10, {}), {3}: (11, {})} | custom-call | tf_op jit(solution)/shard_map/project/pallas_call | solution.py:92
  121.1 8.0 %early_terms.2.term_ref.own_ref = bf16[2,256,1536]{2,1,0:T(8,128)(2,1)} custom-call(bf16[4,256,384]{2,1,0:T(8,128)(2,1)} %get-tuple-element.60.q_ref, bf16[1024,384]{1,0:T(8,128)(2,1)} %bitcast.57, bf16[4,256,768]{2,1,0:T(8,128)(2,1)} %get-tuple-element.62.hidden_ref, bf16[192,1536]{1,0:T(8,128)(2,1)} %out_w.3, bf16[768,1536]{1,0:T(8,128)(2,1)} %down_w.3), custom_call_target="tpu_custom_call" | custom-call | tf_op jit(solution)/shard_map/early_terms/pallas_call | solution.py:163
  133.0 4.8 %collective-permute-done.18.behind_ref = bf16[64,1536]{1,0:T(8,128)(2,1)S(1)} collective-permute-done((bf16[64,1536]{1,0:T(8,128)(2,1)S(1)}, bf16[64,1536]{1,0:T(8,128)(2,1)S(1)}, u32[]{:S(2)}, u32[]{:S(2)}) %collective-permute-start.18) | collective-permute-done | bytes 196640 | tf_op jit(solution)/shard_map/ppermute | solution.py:30
  137.8 3.4 %collective-permute-done.17.ahead_ref = bf16[64,1536]{1,0:T(8,128)(2,1)S(1)} collective-permute-done((bf16[64,1536]{1,0:T(8,128)(2,1)S(1)}, bf16[64,1536]{1,0:T(8,128)(2,1)S(1)}, u32[]{:S(2)}, u32[]{:S(2)}) %collective-permute-start.17) | collective-permute-done | bytes 196640 | tf_op jit(solution)/shard_map/ppermute | solution.py:30
  147.4 8.0 %early_terms.3.term_ref = bf16[2,256,1536]{2,1,0:T(8,128)(2,1)} custom-call(bf16[4,256,384]{2,1,0:T(8,128)(2,1)} %get-tuple-element.60.q_ref, bf16[1024,384]{1,0:T(8,128)(2,1)} %bitcast.58, bf16[4,256,768]{2,1,0:T(8,128)(2,1)} %get-tuple-element.62.hidden_ref, bf16[192,1536]{1,0:T(8,128)(2,1)} %out_w.3, bf16[768,1536]{1,0:T(8,128)(2,1)} %down_w.3), custom_call_target="tpu_custom_call" | custom-call | tf_op jit(solution)/shard_map/early_terms/pallas_call | solution.py:163
  162.4 8.9 %cross_attention.1 = bf16[8,192,128]{2,1,0:T(8,128)(2,1)} custom-call(s32[40]{0:T(128)} %multiply_add_fusion.item_ref, s32[8]{0:T(128)} %dynamic-slice_reduce_fusion.count_ref, s32[1]{0:T(128)} %bitcast.me_ref, bf16[4,256,384]{2,1,0:T(8,128)(2,1)} %get-tuple-element.58.q_ref, bf16[64,128,384]{2,1,0:T(8,128)(2,1)} %bitcast.14.received_ref), custom_call_target="tpu_custom_call" | custom-call | tf_op jit(solution)/shard_map/cross_attention/pallas_call | solution.py:257
  171.2 3.5 %all-to-all-start.1 = ((bf16[8,192,128]{2,1,0:T(8,128)(2,1)}), bf16[8,192,128]{2,1,0:T(8,128)(2,1)S(1)}, u32[]{:S(2)}, u32[]{:S(2)}) async-start(bf16[8,192,128]{2,1,0:T(8,128)(2,1)} %cross_attention.1), calls=%async_computation.1 | async-start | bytes 786432 | tf_op jit(solution)/shard_map/all_to_all | solution.py:423
  181.0 12.5 %collective-permute-done.23.ahead_ref = bf16[128,1536]{1,0:T(8,128)(2,1)S(1)} collective-permute-done((bf16[128,1536]{1,0:T(8,128)(2,1)}, bf16[128,1536]{1,0:T(8,128)(2,1)S(1)}, u32[]{:S(2)}, u32[]{:S(2)}) %collective-permute-start.23) | collective-permute-done | bytes 393248 | tf_op jit(solution)/shard_map/ppermute | solution.py:30
  196.5 5.8 %finish.1 = bf16[128,1536]{1,0:T(8,128)(2,1)} custom-call(s32[2]{0:T(128)} %pad_add_fusion.1.place_ref, bf16[8,192,128]{2,1,0:T(8,128)(2,1)} %copy-done.3, bf16[8,192,768]{2,1,0:T(8,128)(2,1)} %collect.1.mine_ref, bf16[8,192,768]{2,1,0:T(8,128)(2,1)} %copy-done.2, bf16[128,1536]{1,0:T(8,128)(2,1)} %bitcast.83, bf16[128,1536]{1,0:T(8,128)(2,1)} %copy-done.13, ...), custom_call_target="tpu_custom_call" | custom-call | tf_op jit(solution)/shard_map/finish/pallas_call | solution.py:314
  (117 shorter events, 55.3 us)
Async XLA Ops:
  2.4 14.3 %collective-permute-start.4 = (bf16[128,1536]{1,0:T(8,128)(2,1)S(1)}, bf16[128,1536]{1,0:T(8,128)(2,1)S(1)}, u32[]{:S(2)}, u32[]{:S(2)}) collective-permute-start(bf16[128,1536]{1,0:T(8,128)(2,1)S(1)} %fusion.1.refs_0_), channel_id=1, source_target_pairs={{0,7},{1,0},{2,1},{3,2},{4,3},{5,4},{6,5},{7,6},{8,15},{9,8},{10,9... | collective-permute-start | bytes 1179656 | tf_op jit(solution)/shard_map/ppermute | solution.py:30
  8.3 12.1 %collective-permute-start = (bf16[128,1536]{1,0:T(8,128)(2,1)S(1)}, bf16[128,1536]{1,0:T(8,128)(2,1)S(1)}, u32[]{:S(2)}, u32[]{:S(2)}) collective-permute-start(bf16[128,1536]{1,0:T(8,128)(2,1)S(1)} %fusion.1.refs_0_), channel_id=1, source_target_pairs={{0,1},{1,2},{2,3},{3,4},{4,5},{5,6},{6,7},{7,0},{8,9},{9,10},{10,1... | collective-permute-start | bytes 1179656 | tf_op jit(solution)/shard_map/ppermute | solution.py:30
  16.7 11.2 %collective-permute-start.5 = (bf16[128,1536]{1,0:T(8,128)(2,1)S(1)}, bf16[128,1536]{1,0:T(8,128)(2,1)S(1)}, u32[]{:S(2)}, u32[]{:S(2)}) collective-permute-start(bf16[128,1536]{1,0:T(8,128)(2,1)S(1)} %collective-permute-done.4.refs_1_), channel_id=1, source_target_pairs={{0,7},{1,0},{2,1},{3,2},{4,3},{5,4},{6,5},{7,6},{8,15},{9,8},{10,9... | collective-permute-start | bytes 1179656 | tf_op jit(solution)/shard_map/ppermute | solution.py:30
  20.4 11.2 %collective-permute-start.1 = (bf16[128,1536]{1,0:T(8,128)(2,1)S(1)}, bf16[128,1536]{1,0:T(8,128)(2,1)S(1)}, u32[]{:S(2)}, u32[]{:S(2)}) collective-permute-start(bf16[128,1536]{1,0:T(8,128)(2,1)S(1)} %collective-permute-done.refs_0_), channel_id=1, source_target_pairs={{0,1},{1,2},{2,3},{3,4},{4,5},{5,6},{6,7},{7,0},{8,9},{9,10},{10,1... | collective-permute-start | bytes 1179656 | tf_op jit(solution)/shard_map/ppermute | solution.py:30
  27.9 10.4 %collective-permute-start.6 = (bf16[128,1536]{1,0:T(8,128)(2,1)S(1)}, bf16[128,1536]{1,0:T(8,128)(2,1)S(1)}, u32[]{:S(2)}, u32[]{:S(2)}) collective-permute-start(bf16[128,1536]{1,0:T(8,128)(2,1)S(1)} %collective-permute-done.5.refs_1_), channel_id=1, source_target_pairs={{0,7},{1,0},{2,1},{3,2},{4,3},{5,4},{6,5},{7,6},{8,15},{9,8},{10,9... | collective-permute-start | bytes 1179656 | tf_op jit(solution)/shard_map/ppermute | solution.py:30
  31.6 10.4 %collective-permute-start.2 = (bf16[128,1536]{1,0:T(8,128)(2,1)S(1)}, bf16[128,1536]{1,0:T(8,128)(2,1)S(1)}, u32[]{:S(2)}, u32[]{:S(2)}) collective-permute-start(bf16[128,1536]{1,0:T(8,128)(2,1)S(1)} %collective-permute-done.1.refs_0_), channel_id=1, source_target_pairs={{0,1},{1,2},{2,3},{3,4},{4,5},{5,6},{6,7},{7,0},{8,9},{9,10},{10,1... | collective-permute-start | bytes 1179656 | tf_op jit(solution)/shard_map/ppermute | solution.py:30
  38.3 22.6 %collective-permute-start.7 = (bf16[64,1536]{1,0:T(8,128)(2,1)S(1)}, bf16[64,1536]{1,0:T(8,128)(2,1)S(1)}, u32[]{:S(2)}, u32[]{:S(2)}) collective-permute-start(bf16[64,1536]{1,0:T(8,128)(2,1)S(1)} %slice.25), channel_id=1, source_target_pairs={{0,7},{1,0},{2,1},{3,2},{4,3},{5,4},{6,5},{7,6},{8,15},{9,8},{10,9... | collective-permute-start | bytes 589832 | tf_op jit(solution)/shard_map/ppermute | solution.py:30
  42.8 18.1 %collective-permute-start.3 = (bf16[64,1536]{1,0:T(8,128)(2,1)}, bf16[64,1536]{1,0:T(8,128)(2,1)S(1)}, u32[]{:S(2)}, u32[]{:S(2)}) collective-permute-start(bf16[64,1536]{1,0:T(8,128)(2,1)} %slice.24), channel_id=1, source_target_pairs={{0,1},{1,2},{2,3},{3,4},{4,5},{5,6},{6,7},{7,0},{8,9},{9,10},{10,1... | collective-permute-start | bytes 589832 | tf_op jit(solution)/shard_map/ppermute | solution.py:30
  67.9 94.4 %all-to-all-start = ((bf16[32,2,128,384]{3,2,1,0:T(8,128)(2,1)}), bf16[32,2,128,384]{3,2,1,0:T(8,128)(2,1)}, u32[]{:S(2)}, u32[]{:S(2)}) async-start(bf16[32,2,128,384]{3,2,1,0:T(8,128)(2,1)} %pack_items.1), calls=%async_computation | async-start | bytes 12582912 | tf_op jit(solution)/shard_map/all_to_all | solution.py:397
  75.7 10.6 %collective-permute-start.11 = (bf16[192,768]{1,0:T(8,128)(2,1)S(1)}, bf16[192,768]{1,0:T(8,128)(2,1)S(1)}, u32[]{:S(2)}, u32[]{:S(2)}) collective-permute-start(bf16[192,768]{1,0:T(8,128)(2,1)S(1)} %constant_dynamic-slice_fusion.refs_0_), channel_id=1, source_target_pairs={{0,1},{1,2},{2,3},{3,4},{4,5},{5,6},{6,7},{7,0},{8,9},{9,10},{10,1... | collective-permute-start | bytes 884744 | tf_op jit(solution)/shard_map/ppermute | solution.py:30
  75.8 10.5 %collective-permute-start.8 = (bf16[192,768]{1,0:T(8,128)(2,1)S(1)}, bf16[192,768]{1,0:T(8,128)(2,1)S(1)}, u32[]{:S(2)}, u32[]{:S(2)}) collective-permute-start(bf16[192,768]{1,0:T(8,128)(2,1)S(1)} %constant_dynamic-slice_fusion.refs_0_), channel_id=1, source_target_pairs={{0,7},{1,0},{2,1},{3,2},{4,3},{5,4},{6,5},{7,6},{8,15},{9,8},{10,9... | collective-permute-start | bytes 884744 | tf_op jit(solution)/shard_map/ppermute | solution.py:30
  86.3 9.8 %collective-permute-start.12 = (bf16[192,768]{1,0:T(8,128)(2,1)S(1)}, bf16[192,768]{1,0:T(8,128)(2,1)S(1)}, u32[]{:S(2)}, u32[]{:S(2)}) collective-permute-start(bf16[192,768]{1,0:T(8,128)(2,1)S(1)} %collective-permute-done.11.refs_8_), channel_id=1, source_target_pairs={{0,1},{1,2},{2,3},{3,4},{4,5},{5,6},{6,7},{7,0},{8,9},{9,10},{10,1... | collective-permute-start | bytes 884744 | tf_op jit(solution)/shard_map/ppermute | solution.py:30
  86.3 9.8 %collective-permute-start.9 = (bf16[192,768]{1,0:T(8,128)(2,1)S(1)}, bf16[192,768]{1,0:T(8,128)(2,1)S(1)}, u32[]{:S(2)}, u32[]{:S(2)}) collective-permute-start(bf16[192,768]{1,0:T(8,128)(2,1)S(1)} %collective-permute-done.8.refs_1_), channel_id=1, source_target_pairs={{0,7},{1,0},{2,1},{3,2},{4,3},{5,4},{6,5},{7,6},{8,15},{9,8},{10,9... | collective-permute-start | bytes 884744 | tf_op jit(solution)/shard_map/ppermute | solution.py:30
  96.1 9.0 %collective-permute-start.13 = (bf16[192,768]{1,0:T(8,128)(2,1)S(1)}, bf16[192,768]{1,0:T(8,128)(2,1)S(1)}, u32[]{:S(2)}, u32[]{:S(2)}) collective-permute-start(bf16[192,768]{1,0:T(8,128)(2,1)S(1)} %collective-permute-done.12.refs_7_), channel_id=1, source_target_pairs={{0,1},{1,2},{2,3},{3,4},{4,5},{5,6},{6,7},{7,0},{8,9},{9,10},{10,1... | collective-permute-start | bytes 884744 | tf_op jit(solution)/shard_map/ppermute | solution.py:30
  96.1 9.1 %collective-permute-start.10 = (bf16[192,768]{1,0:T(8,128)(2,1)S(1)}, bf16[192,768]{1,0:T(8,128)(2,1)S(1)}, u32[]{:S(2)}, u32[]{:S(2)}) collective-permute-start(bf16[192,768]{1,0:T(8,128)(2,1)S(1)} %collective-permute-done.9.refs_2_), channel_id=1, source_target_pairs={{0,7},{1,0},{2,1},{3,2},{4,3},{5,4},{6,5},{7,6},{8,15},{9,8},{10,9... | collective-permute-start | bytes 884744 | tf_op jit(solution)/shard_map/ppermute | solution.py:30
  116.0 79.0 %collective-permute-start.16 = (bf16[8,192,768]{2,1,0:T(8,128)(2,1)}, bf16[8,192,768]{2,1,0:T(8,128)(2,1)S(1)}, u32[]{:S(2)}, u32[]{:S(2)}) collective-permute-start(bf16[8,192,768]{2,1,0:T(8,128)(2,1)} %collect.1.mine_ref), channel_id=1, source_target_pairs={{0,8},{8,0},{16,24},{24,16},{32,40},{40,32},{48,56},{56,48},{64,72... | collective-permute-start | bytes 7077896 | tf_op jit(solution)/shard_map/ppermute | solution.py:410
  133.0 8.2 %collective-permute-start.17 = (bf16[64,1536]{1,0:T(8,128)(2,1)S(1)}, bf16[64,1536]{1,0:T(8,128)(2,1)S(1)}, u32[]{:S(2)}, u32[]{:S(2)}) collective-permute-start(bf16[64,1536]{1,0:T(8,128)(2,1)S(1)} %get-tuple-element.72), channel_id=1, source_target_pairs={{0,1},{1,2},{2,3},{3,4},{4,5},{5,6},{6,7},{7,0},{8,9},{9,10},{10,1... | collective-permute-start | bytes 589832 | tf_op jit(solution)/shard_map/ppermute | solution.py:30
  144.2 11.8 %collective-permute-start.19 = (bf16[128,1536]{1,0:T(8,128)(2,1)}, bf16[128,1536]{1,0:T(8,128)(2,1)S(1)}, u32[]{:S(2)}, u32[]{:S(2)}) collective-permute-start(bf16[128,1536]{1,0:T(8,128)(2,1)} %get-tuple-element.63), channel_id=1, source_target_pairs={{0,1},{1,2},{2,3},{3,4},{4,5},{5,6},{6,7},{7,0},{8,9},{9,10},{10,1... | collective-permute-start | bytes 1179656 | tf_op jit(solution)/shard_map/ppermute | solution.py:30
  144.2 11.8 %collective-permute-start.20 = (bf16[128,1536]{1,0:T(8,128)(2,1)}, bf16[128,1536]{1,0:T(8,128)(2,1)}, u32[]{:S(2)}, u32[]{:S(2)}) collective-permute-start(bf16[128,1536]{1,0:T(8,128)(2,1)} %get-tuple-element.64), channel_id=1, source_target_pairs={{0,7},{1,0},{2,1},{3,2},{4,3},{5,4},{6,5},{7,6},{8,15},{9,8},{10,9... | collective-permute-start | bytes 1179656 | tf_op jit(solution)/shard_map/ppermute | solution.py:30
  159.1 15.6 %collective-permute-start.21 = (bf16[128,1536]{1,0:T(8,128)(2,1)}, bf16[128,1536]{1,0:T(8,128)(2,1)}, u32[]{:S(2)}, u32[]{:S(2)}) collective-permute-start(bf16[128,1536]{1,0:T(8,128)(2,1)} %get-tuple-element.65), channel_id=1, source_target_pairs={{0,1},{1,2},{2,3},{3,4},{4,5},{5,6},{6,7},{7,0},{8,9},{9,10},{10,1... | collective-permute-start | bytes 1179656 | tf_op jit(solution)/shard_map/ppermute | solution.py:30
  159.1 15.6 %collective-permute-start.22 = (bf16[128,1536]{1,0:T(8,128)(2,1)}, bf16[128,1536]{1,0:T(8,128)(2,1)}, u32[]{:S(2)}, u32[]{:S(2)}) collective-permute-start(bf16[128,1536]{1,0:T(8,128)(2,1)} %get-tuple-element.66), channel_id=1, source_target_pairs={{0,7},{1,0},{2,1},{3,2},{4,3},{5,4},{6,5},{7,6},{8,15},{9,8},{10,9... | collective-permute-start | bytes 1179656 | tf_op jit(solution)/shard_map/ppermute | solution.py:30
  171.2 23.8 %all-to-all-start.1 = ((bf16[8,192,128]{2,1,0:T(8,128)(2,1)}), bf16[8,192,128]{2,1,0:T(8,128)(2,1)S(1)}, u32[]{:S(2)}, u32[]{:S(2)}) async-start(bf16[8,192,128]{2,1,0:T(8,128)(2,1)} %cross_attention.1), calls=%async_computation.1 | async-start | bytes 786432 | tf_op jit(solution)/shard_map/all_to_all | solution.py:423
  177.1 16.4 %collective-permute-start.23 = (bf16[128,1536]{1,0:T(8,128)(2,1)}, bf16[128,1536]{1,0:T(8,128)(2,1)S(1)}, u32[]{:S(2)}, u32[]{:S(2)}) collective-permute-start(bf16[128,1536]{1,0:T(8,128)(2,1)} %get-tuple-element.67), channel_id=1, source_target_pairs={{0,1},{1,2},{2,3},{3,4},{4,5},{5,6},{6,7},{7,0},{8,9},{9,10},{10,1... | collective-permute-start | bytes 1179656 | tf_op jit(solution)/shard_map/ppermute | solution.py:30
  179.0 14.5 %collective-permute-start.24 = (bf16[128,1536]{1,0:T(8,128)(2,1)}, bf16[128,1536]{1,0:T(8,128)(2,1)S(1)}, u32[]{:S(2)}, u32[]{:S(2)}) collective-permute-start(bf16[128,1536]{1,0:T(8,128)(2,1)} %get-tuple-element.68), channel_id=1, source_target_pairs={{0,7},{1,0},{2,1},{3,2},{4,3},{5,4},{6,5},{7,6},{8,15},{9,8},{10,9... | collective-permute-start | bytes 1179656 | tf_op jit(solution)/shard_map/ppermute | solution.py:30
  (29 other events, 380.1 us)

commit v2 on v1

--- a/solution.py
+++ b/solution.py
@@ -41,6 +41,29 @@
     return pair_heads(queries, jnp.zeros_like(queries))
 
 
+def params(mebibytes):
+    return pltpu.CompilerParams(vmem_limit_bytes=mebibytes << 20)
+
+
+def split(array, at, first, count):
+    half = count // 2
+
+    def kernel(ref, top_ref, low_ref):
+        block = ref.at[at] if array.ndim == 3 else ref
+        top_ref[...] = block[first : first + half]
+        low_ref[...] = block[first + half : first + count]
+
+    vmem = pl.BlockSpec(memory_space=pltpu.VMEM)
+    return pl.pallas_call(
+        kernel,
+        in_specs=[vmem],
+        out_specs=[vmem, vmem],
+        out_shape=[jax.ShapeDtypeStruct((half, array.shape[-1]), BF16)] * 2,
+        compiler_params=params(12),
+        name="split",
+    )(array)
+
+
 def dot(a, b):
     return jnp.dot(a, b, preferred_element_type=F32)
 
@@ -64,19 +87,24 @@
 def project_rows(x, weights, outs):
     sq, sk, sv, cq, up, ck, cv = weights
     self_q, self_kv, cross_q, hidden = outs[:4]
+
+    def put(out, value):
+        out[...] = value.reshape(out.shape)
+
     if ck is not None:
-        outs[4][0] = pair_heads(dot_rows(x, ck[...]), dot_rows(x, cv[...]))
-    self_kv[0] = pair_heads(dot_rows(x, sk[...]), dot_rows(x, sv[...]))
-    self_q[0] = pad_heads(dot_rows(x, sq[...]))
-    cross_q[0] = pad_heads(dot_rows(x, cq[...]))
-    hidden[0] = jax.nn.gelu(dot(x, up[...])).astype(BF16)
+        put(outs[4], pair_heads(dot_rows(x, ck[...]), dot_rows(x, cv[...])))
+    put(self_kv, pair_heads(dot_rows(x, sk[...]), dot_rows(x, sv[...])))
+    put(self_q, pad_heads(dot_rows(x, sq[...])))
+    put(cross_q, pad_heads(dot_rows(x, cq[...])))
+    put(hidden, jax.nn.gelu(dot(x, up[...])).astype(BF16))
 
 
 def project(blocks, weights, held, place, with_cross):
     sq, sk, sv, cq, up, ck, cv = weights
     operands = [*blocks, sq, sk, sv, cq, up] + ([ck, cv] if with_cross else [])
     count = len(blocks)
-    rows = sum(block.shape[0] for block in blocks)
+    depth, both = 4, 2 * blocks[0].shape[0]
+    per = sum(block.shape[0] for block in blocks) // both
     cols, ff = sq.shape[0], up.shape[1]
     widths = [2 * cols, 2 * cols, 2 * cols, ff] + ([2 * cols] if with_cross else [])
     n_held = 0 if held is None else len(held)
@@ -88,58 +116,74 @@
             inputs += [None, None]
         project_rows(x, inputs, refs[len(operands) + n_held :])
 
-    depth = 4
     return pl.pallas_call(
         kernel,
         grid=(1,),
         in_specs=[whole(a) for a in operands] + [pl.BlockSpec(memory_space=pl.ANY)] * n_held,
-        out_specs=[pl.BlockSpec((1, rows, n), lambda i: (place, 0, 0)) for n in widths],
-        out_shape=[jax.ShapeDtypeStruct((depth, rows, n), BF16) for n in widths],
+        out_specs=[pl.BlockSpec((per, both, n), lambda i: (place, 0, 0)) for n in widths],
+        out_shape=[jax.ShapeDtypeStruct((depth, both, n), BF16) for n in widths],
         input_output_aliases={len(operands) + i: i for i in range(n_held)},
         name="project",
     )(*operands, *([] if held is None else held))
 
 
-def pack_items(table, blocks, paired, ck, cv, capacity):
-    count = len(blocks)
+def cross_pairs(blocks, ck, cv, paired):
+    rows = blocks[0].shape[0]
+    _, both, width = paired.shape
+
+    def kernel(up_ref, down_ref, own_ref, ck_ref, cv_ref, _, out_ref):
+        x = jnp.concatenate([up_ref[...], down_ref[...], own_ref[...]], 0)
+        last = pair_heads(dot_rows(x, ck_ref[...]), dot_rows(x, cv_ref[...]))
+        out_ref[0] = last[:both]
+        out_ref[1, :rows] = last[both:]
+        out_ref[1, rows:] = jnp.zeros((rows, width), BF16)
+
+    operands = (*blocks, ck, cv)
+    return pl.pallas_call(
+        kernel,
+        grid=(1,),
+        in_specs=[whole(a) for a in operands] + [pl.BlockSpec(memory_space=pl.ANY)],
+        out_specs=pl.BlockSpec((2, both, width), lambda i: (1, 0, 0)),
+        out_shape=jax.ShapeDtypeStruct(paired.shape, BF16),
+        input_output_aliases={len(operands): 0},
+        name="cross_pairs",
+    )(*operands, paired)
+
+
+def pack_items(table, far, paired, ck, cv, n_view, capacity):
     depth, both, width = paired.shape
     rows = both // 2
-    items = table.shape[0]
-    n_view = items // capacity
-    steps = 4
+    steps = 8
     block = n_view // steps
 
-    def kernel(table_ref, *refs):
-        xs, (pair_ref, ck_ref, cv_ref, out_ref, held) = refs[:count], refs[count:]
+    def kernel(table_ref, top_ref, low_ref, pair_ref, ck_ref, cv_ref, out_ref, held):
         step = pl.program_id(0)
 
         @pl.when(step == 0)
         def _():
-            x = jnp.concatenate([ref[...] for ref in xs], 0)
-            last = pair_heads(dot_rows(x, ck_ref[...]), dot_rows(x, cv_ref[...]))
-            held[2 * depth - 2] = last[:rows]
-            held[2 * depth - 1] = last[rows:]
-            for k in range(depth - 1):
-                held[2 * k] = pair_ref[k, :rows]
-                held[2 * k + 1] = pair_ref[k, rows:]
+            x = jnp.concatenate([top_ref[...], low_ref[...]], 0)
+            held[2 * depth - 1] = pair_heads(dot_rows(x, ck_ref[...]), dot_rows(x, cv_ref[...]))
+            for slot in range(2 * depth - 1):
+                half = slot % 2
+                held[slot] = pair_ref[slot // 2, half * rows : (half + 1) * rows]
 
         for i in range(block):
             for j in range(capacity):
                 out_ref[i, j] = held[table_ref[j * n_view + step * block + i]]
 
+    operands = (*far, paired, ck, cv)
     return pl.pallas_call(
         kernel,
         grid_spec=pltpu.PrefetchScalarGridSpec(
             num_scalar_prefetch=1,
             grid=(steps,),
-            in_specs=[whole(x) for x in blocks]
-            + [pl.BlockSpec((depth - 1, both, width), lambda i, t: (0, 0, 0)), whole(ck), whole(cv)],
+            in_specs=[whole(a) for a in operands],
             out_specs=pl.BlockSpec((block, capacity, rows, width), lambda i, t: (i, 0, 0, 0)),
             scratch_shapes=[pltpu.VMEM((2 * depth, rows, width), BF16)],
         ),
         out_shape=jax.ShapeDtypeStruct((n_view, capacity, rows, width), BF16),
         name="pack_items",
-    )(table, *blocks, paired, ck, cv)
+    )(table, *operands)
 
 
 def early_kernel(q_ref, kv_ref, hidden_ref, out_w, down_w, result):
@@ -172,6 +216,7 @@
         ],
         out_specs=pl.BlockSpec((1, rows, cols), lambda i: (i, 0, 0)),
         out_shape=jax.ShapeDtypeStruct((count, rows, cols), BF16),
+        compiler_params=params(24),
         name="early_terms",
     )(q, kv, hidden, out_w, down_w)
 
@@ -200,6 +245,7 @@
         in_specs=[whole(ahead), whole(behind), pl.BlockSpec((1, *terms.shape[1:]), lambda i: (at, 0, 0))],
         out_specs=[pl.BlockSpec(shape.shape, lambda i: (0, 0))] * 2,
         out_shape=[shape, shape],
+        compiler_params=params(12),
         name="add_pair",
     )(ahead, behind, terms)
 
@@ -263,6 +309,7 @@
             pltpu.VMEM((strips, SLOTS * rows, width), BF16),
             pltpu.SemaphoreType.DMA((strips, SLOTS)),
         ],
+        compiler_params=params(20),
         name="cross_attention",
     )(items, counts, me, q, received)
 
@@ -285,31 +332,51 @@
         in_specs=[vmem] * len(blocks),
         out_specs=vmem,
         out_shape=jax.ShapeDtypeStruct((strips, rows, cols), BF16),
+        compiler_params=params(12),
         name="collect",
     )(*blocks)
 
 
-def finish(place, mix, mine, other, token_rows, ahead, behind, terms, at):
+def earlier(token_rows, ahead, behind, terms, at):
+    rows, cols = token_rows.shape
+
+    def kernel(token_ref, ahead_ref, behind_ref, own_ref, out_ref):
+        early = ahead_ref[...].astype(F32) + behind_ref[...].astype(F32) + own_ref[0].astype(F32)
+        out_ref[...] = token_ref[...].astype(F32) + early
+
+    return pl.pallas_call(
+        kernel,
+        grid=(1,),
+        in_specs=[
+            whole(token_rows),
+            whole(ahead),
+            whole(behind),
+            pl.BlockSpec((1, rows, cols), lambda i: (at, 0, 0)),
+        ],
+        out_specs=whole(token_rows),
+        out_shape=jax.ShapeDtypeStruct((rows, cols), F32),
+        compiler_params=params(12),
+        name="earlier",
+    )(token_rows, ahead, behind, terms)
+
+
+def finish(place, mix, mine, other, base):
     strips, width, half = mine.shape
-    rows = token_rows.shape[0]
     cols = 256
 
-    def kernel(place_ref, mix_ref, mine_ref, other_ref, token_ref, ahead_ref, behind_ref, own_ref, out_ref):
+    def kernel(place_ref, mix_ref, mine_ref, other_ref, base_ref, out_ref, turned):
         me, side = place_ref[0], place_ref[1]
         step = pl.program_id(0)
+
+        @pl.when(step == 0)
+        def _():
+            for j in range(strips):
+                turned[:, j * width : (j + 1) * width] = mix_ref[lax.rem(me + j, strips)].T
+
         for weights, part in ((mine_ref, side), (other_ref, 1 - side)):
-            total = 0.0
-            for j in range(strips):
-                total = total + lax.dot_general(
-                    mix_ref[lax.rem(me + j, strips)],
-                    weights[j],
-                    (((0,), (0,)), ((), ())),
-                    preferred_element_type=F32,
-                )
+            total = dot(turned[...], weights[...].reshape(strips * width, cols))
             here = pl.ds(pl.multiple_of(part * half + step * cols, 128), cols)
-            early = ahead_ref[:, here].astype(F32) + behind_ref[:, here].astype(F32)
-            early = early + own_ref[0, :, here].astype(F32)
-            out_ref[:, here] = (token_ref[:, here].astype(F32) + (total + early)).astype(BF16)
+            out_ref[:, here] = (base_ref[:, here] + total).astype(BF16)
 
     return pl.pallas_call(
         kernel,
@@ -320,16 +387,15 @@
                 whole(mix),
                 pl.BlockSpec((strips, width, cols), lambda i, p: (0, 0, i)),
                 pl.BlockSpec((strips, width, cols), lambda i, p: (0, 0, i)),
-                whole(token_rows),
-                whole(ahead),
-                whole(behind),
-                pl.BlockSpec((1, rows, terms.shape[2]), lambda i, p: (at, 0, 0)),
+                whole(base),
             ],
-            out_specs=whole(token_rows),
+            out_specs=whole(base),
+            scratch_shapes=[pltpu.VMEM((mix.shape[2], strips * width), BF16)],
         ),
-        out_shape=jax.ShapeDtypeStruct(token_rows.shape, BF16),
+        out_shape=jax.ShapeDtypeStruct(base.shape, BF16),
+        compiler_params=params(24),
         name="finish",
-    )(place, mix, mine, other, token_rows, ahead, behind, terms)
+    )(place, mix, mine, other, base)
 
 
 def routing(source_ids, source_count, my_view, my_strip, n_view, n_strip):
@@ -374,7 +440,9 @@
     side = my_view % 2
     capacity = 2
     routes = routing(source_ids, source_count, my_view, my_strip, n_view, n_strip)
-    table, items, counts = lax.optimization_barrier(routes)
+    half = cross_out.shape[1] // 2
+    my_half = lax.dynamic_slice_in_dim(cross_out, side * half, half, 1)
+    place = jnp.stack([my_strip, side]).astype(jnp.int32)
 
     weights = [self_query.T, self_key.T, self_value.T, cross_query.T, mlp_up, cross_key.T, cross_value.T]
 
@@ -385,43 +453,44 @@
     half_rows = normed.shape[0] // 2
     ahead, behind, held = normed, normed, None
     ahead, behind = both(ahead, behind)
-    for step in range(3):
-        pair = [ahead, behind]
-        if step < 2:
-            ahead, behind = both(ahead, behind)
-        else:
-            ahead, behind = both(ahead[:half_rows], behind[half_rows:])
+    early_ahead, routes, my_half, place = lax.optimization_barrier((ahead, routes, my_half, place))
+    table, items, counts = routes
+    for step in range(2):
+        pair = [ahead if step else early_ahead, behind]
+        ahead, behind = both(ahead, behind)
         held = project(pair, weights, held, step, True)
-    blocks = [normed, ahead, behind]
-    outgoing = pack_items(table, blocks, held[4], weights[5], weights[6], capacity)
+    pair = [ahead, behind]
+    far = both(ahead[:half_rows], behind[half_rows:])
+    paired = cross_pairs([*pair, normed], weights[5], weights[6], held[4])
+    outgoing = pack_items(table, far, paired, weights[5], weights[6], n_view, capacity)
+    blocks = [*pair, normed, *far]
     received = lax.all_to_all(outgoing, "view", split_axis=0, concat_axis=0, tiled=True)
     received = received.reshape(n_view * capacity, *outgoing.shape[2:])
 
-    half = cross_out.shape[1] // 2
-    my_half = lax.dynamic_slice_in_dim(cross_out, side * half, half, 1)
     my_half, outgoing, blocks = lax.optimization_barrier((my_half, outgoing, blocks))
     ahead, behind, found = my_half, my_half, {0: my_half}
     for step in range(1, 4):
         ahead, behind = both(ahead, behind)
         found[n_strip - step], found[step] = ahead, behind
     part = my_half.shape[0] // 2
-    far = both(ahead[:part], behind[part:])
-    my_halves = collect([found[j] for j in range(n_strip) if j != n_strip // 2], far)
+    rest = both(ahead[:part], behind[part:])
+    my_halves = collect([found[j] for j in range(n_strip) if j != n_strip // 2], rest)
     other_halves = lax.ppermute(my_halves, "view", [(i, i ^ 1) for i in range(n_view)])
 
-    self_q, self_kv, cross_q, hidden = project(blocks, weights, held[:4], 3, False)
+    self_q, self_kv, cross_q, hidden = project(blocks, weights, held[:4], 1, False)
     late = early_terms(self_q, self_kv, hidden, self_out, mlp_down, 2, 2)
-    soon = early_terms(self_q, self_kv, hidden, self_out, mlp_down, 0, 2)
+    soon = early_terms(self_q, self_kv, hidden, self_out, mlp_down, 1, 1)
+    last = early_terms(self_q, self_kv, hidden, self_out, mlp_down, 0, 1)
     rows = normed.shape[0]
-    ahead, behind = both(late[1, rows : rows + half_rows], late[1, rows + half_rows :])
-    for terms, at in ((late, 0), (soon, 1), (soon, 0)):
+    ahead, behind = both(*split(late, 1, rows, rows))
+    for terms, at in ((late, 0), (soon, 0), (last, 0)):
         ahead, behind = add_pair(ahead, behind, terms, at)
         ahead, behind = both(ahead, behind)
 
-    place = jnp.stack([my_strip, side]).astype(jnp.int32)
     cross_mix = cross_attention(items, counts, place[:1], cross_q, received, n_strip)
     cross_mix = lax.all_to_all(cross_mix, "strip", split_axis=0, concat_axis=0, tiled=True)
-    return finish(place, cross_mix, my_halves, other_halves, tokens[0], ahead, behind, late, 1)[None]
+    base = earlier(tokens[0], ahead, behind, late, 1)
+    return finish(place, cross_mix, my_halves, other_halves, base)[None]
 
 
 def solution(mesh):

time: 203 us -> 193 us (0.951)
  Pallas kernels: 69.7 us -> 55.7 us
    pallas_call x2 -> x3, Pallas kernels: 16.1 us -> 9.51 us  [early_terms(): pl.pallas_call(early_kernel, grid=(count,), in_specs=[pl.BlockSpec((1, ro...]
    pallas_call x3, Pallas kernels: 6.97 us -> 2.5 us  [add_pair(): pl.pallas_call(kernel, grid=(1,), in_specs=[whole(ahead), whole(behind),...]
    pallas_call x4 -> x3, Pallas kernels: 22.6 us -> 18.8 us  [project(): pl.pallas_call(kernel, grid=(1,), in_specs=[whole(a) for a in operands] +...]
    pallas_call x0 -> x3, Pallas kernels: none -> 3.42 us  [the longest x1 3.21 us: cross_pairs(): pl.pallas_call(kernel, grid=(1,), in_specs=[whole(a) for a in operands] +...]
    unnamed x53 -> x49, local copies, waits for them, and re-layouts: 6.53 us -> 9.82 us
  transfers between devices with their start and end apart: 27 -> 27, of which waited for: 11 -> 10; matrix products, arithmetic and copies ran while one was open for 3% -> 2% of each run, Pallas kernels for 28% -> 23%
where the time goes in v2:
time: 193 us; the launch traced here: 192 us
  waiting for transfers between devices  63.7 us (33%)
  starting transfers between devices  55.8 us (29%)
  Pallas kernels  55.7 us (29%)
  local copies, waits for them, and re-layouts  12.3 us (6%)
  other arithmetic  3.96 us (2%)
    ppermute x24, waiting for transfers between devices, shift(): return lax.ppermute(value, 'strip', ring_pairs(size, step))  63.7 us
    ppermute x24, starting transfers between devices, shift(): return lax.ppermute(value, 'strip', ring_pairs(size, step))  44.2 us
    pallas_call x3, Pallas kernels, project(): pl.pallas_call(kernel, grid=(1,), in_specs=[whole(a) for a in operands] +...  18.8 us
    unnamed x49, local copies, waits for them, and re-layouts  9.82 us
    pallas_call x3, Pallas kernels, early_terms(): pl.pallas_call(early_kernel, grid=(count,), in_specs=[pl.BlockSpec((1, ro...  9.51 us
    pallas_call x1, Pallas kernels, cross_attention(): pl.pallas_call(kernel, in_specs=[smem, smem, smem, pl.BlockSpec(memory_sp...  7.66 us
    all_to_all x1, starting transfers between devices, per_device(): lax.all_to_all(outgoing, 'view', split_axis=0, concat_axis=0, tiled=True)  7.55 us
    pallas_call x1, Pallas kernels, pack_items(): pl.pallas_call(kernel, grid_spec=pltpu.PrefetchScalarGridSpec(num_scalar_...  7.07 us
  transfers between devices with their start and end apart: 27, of which 10 were waited for; matrix products, arithmetic and copies ran while one was open for 2% of the time, Pallas kernels for 23%

profile of v2, /device:TPU:12, one launch (start us, length us, event | category | flops | bytes accessed | tf_op | source)
XLA Modules:
  0.0 191.9 jit_solution(78594491534355037)
XLA Ops:
  2.4 5.9 %collective-permute-start.4 = (bf16[128,1536]{1,0:T(8,128)(2,1)S(1)}, bf16[128,1536]{1,0:T(8,128)(2,1)S(1)}, u32[]{:S(2)}, u32[]{:S(2)}) collective-permute-start(bf16[128,1536]{1,0:T(8,128)(2,1)S(1)} %fusion.1.own_ref.refs_2_), channel_id=1, source_target_pairs={{0,7},{1,0},{2,1},{3,2},{4,3},{5,4},{6,5},{7,6},{8,15},{9,8},{10,9... | collective-permute-start | bytes 1179656 | tf_op jit(solution)/shard_map/ppermute | solution.py:30
  10.0 6.7 %collective-permute-done.4.refs_1_ = bf16[128,1536]{1,0:T(8,128)(2,1)S(1)} collective-permute-done((bf16[128,1536]{1,0:T(8,128)(2,1)S(1)}, bf16[128,1536]{1,0:T(8,128)(2,1)S(1)}, u32[]{:S(2)}, u32[]{:S(2)}) %collective-permute-start.4) | collective-permute-done | bytes 393248 | tf_op jit(solution)/shard_map/ppermute | solution.py:30
  16.7 3.7 %collective-permute-start.5 = (bf16[128,1536]{1,0:T(8,128)(2,1)S(1)}, bf16[128,1536]{1,0:T(8,128)(2,1)S(1)}, u32[]{:S(2)}, u32[]{:S(2)}) collective-permute-start(bf16[128,1536]{1,0:T(8,128)(2,1)S(1)} %collective-permute-done.4.refs_1_), channel_id=1, source_target_pairs={{0,7},{1,0},{2,1},{3,2},{4,3},{5,4},{6,5},{7,6},{8,15},{9,8},{10,9... | collective-permute-start | bytes 1179656 | tf_op jit(solution)/shard_map/ppermute | solution.py:30
  20.6 7.3 %collective-permute-done.5.refs_1_ = bf16[128,1536]{1,0:T(8,128)(2,1)S(1)} collective-permute-done((bf16[128,1536]{1,0:T(8,128)(2,1)S(1)}, bf16[128,1536]{1,0:T(8,128)(2,1)S(1)}, u32[]{:S(2)}, u32[]{:S(2)}) %collective-permute-start.5) | collective-permute-done | bytes 393248 | tf_op jit(solution)/shard_map/ppermute | solution.py:30
  27.9 3.7 %collective-permute-start.6 = (bf16[128,1536]{1,0:T(8,128)(2,1)S(1)}, bf16[128,1536]{1,0:T(8,128)(2,1)S(1)}, u32[]{:S(2)}, u32[]{:S(2)}) collective-permute-start(bf16[128,1536]{1,0:T(8,128)(2,1)S(1)} %collective-permute-done.5.refs_1_), channel_id=1, source_target_pairs={{0,7},{1,0},{2,1},{3,2},{4,3},{5,4},{6,5},{7,6},{8,15},{9,8},{10,9... | collective-permute-start | bytes 1179656 | tf_op jit(solution)/shard_map/ppermute | solution.py:30
  32.8 5.5 %collective-permute-done.6.down_ref.refs_1_ = bf16[128,1536]{1,0:T(8,128)(2,1)S(1)} collective-permute-done((bf16[128,1536]{1,0:T(8,128)(2,1)S(1)}, bf16[128,1536]{1,0:T(8,128)(2,1)S(1)}, u32[]{:S(2)}, u32[]{:S(2)}) %collective-permute-start.6) | collective-permute-done | bytes 393248 | tf_op jit(solution)/shard_map/ppermute | solution.py:30
  38.3 3.8 %collective-permute-start.7 = (bf16[64,1536]{1,0:T(8,128)(2,1)S(1)}, bf16[64,1536]{1,0:T(8,128)(2,1)S(1)}, u32[]{:S(2)}, u32[]{:S(2)}) collective-permute-start(bf16[64,1536]{1,0:T(8,128)(2,1)S(1)} %slice.21), channel_id=1, source_target_pairs={{0,7},{1,0},{2,1},{3,2},{4,3},{5,4},{6,5},{7,6},{8,15},{9,8},{10,9... | collective-permute-start | bytes 589832 | tf_op jit(solution)/shard_map/ppermute | solution.py:30
  43.3 5.8 %project.3 = (bf16[4,256,384]{2,1,0:T(8,128)(2,1)}, bf16[4,256,384]{2,1,0:T(8,128)(2,1)}, bf16[4,256,384]{2,1,0:T(8,128)(2,1)}, bf16[4,256,768]{2,1,0:T(8,128)(2,1)}, bf16[4,256,384]{2,1,0:T(8,128)(2,1)}) custom-call(bf16[128,1536]{1,0:T(8,128)(2,1)} %copy-done.23, bf16[128,1536]{1,0:T(8,128)(2,1)} %copy-done.22, bf16[192,1536]{1,0:T(8,128)(2,1)} %bitcast.67, ...), custom_call_target="tpu_custom_call" | custom-call | tf_op jit(solution)/shard_map/project/pallas_call | solution.py:119
  49.2 5.8 %project.4 = (bf16[4,256,384]{2,1,0:T(8,128)(2,1)}, bf16[4,256,384]{2,1,0:T(8,128)(2,1)}, bf16[4,256,384]{2,1,0:T(8,128)(2,1)}, bf16[4,256,768]{2,1,0:T(8,128)(2,1)}, bf16[4,256,384]{2,1,0:T(8,128)(2,1)}) custom-call(bf16[128,1536]{1,0:T(8,128)(2,1)} %copy-done.21, ...), custom_call_target="tpu_custom_call", output_to_operand_aliasing={{0}: (9, {}), {1}: (10, {}), {2}: (11, {}), {3}: (12, {}), ... | custom-call | tf_op jit(solution)/shard_map/project/pallas_call | solution.py:119
  59.6 7.1 %pack_items.1 = bf16[32,2,128,384]{3,2,1,0:T(8,128)(2,1)} custom-call(s32[64]{0:T(128)} %compare_select_fusion.6.table_ref, bf16[64,1536]{1,0:T(8,128)(2,1)} %copy-done.19, bf16[64,1536]{1,0:T(8,128)(2,1)} %copy-done.18, bf16[4,256,384]{2,1,0:T(8,128)(2,1)} %cross_pairs.1.pair_ref, bf16[192,1536]{1,0:T(8,128)(2,1)} %bitcast.62, bf16[192,1536]{1,0:T(8,128)(2,1)} %bitcast.66), custom_call_target="tpu_custom_call" | custom-call | tf_op jit(solution)/shard_map/pack_items/pallas_call | solution.py:175
  66.7 7.5 %all-to-all-start = ((bf16[32,2,128,384]{3,2,1,0:T(8,128)(2,1)}), bf16[32,2,128,384]{3,2,1,0:T(8,128)(2,1)}, u32[]{:S(2)}, u32[]{:S(2)}) async-start(bf16[32,2,128,384]{3,2,1,0:T(8,128)(2,1)} %pack_items.1), calls=%async_computation | async-start | bytes 12582912 | tf_op jit(solution)/shard_map/all_to_all | solution.py:467
  74.3 3.5 %collective-permute-start.8 = (bf16[192,768]{1,0:T(8,128)(2,1)S(1)}, bf16[192,768]{1,0:T(8,128)(2,1)S(1)}, u32[]{:S(2)}, u32[]{:S(2)}) collective-permute-start(bf16[192,768]{1,0:T(8,128)(2,1)S(1)} %constant_dynamic-slice_fusion.refs_0_), channel_id=1, source_target_pairs={{0,7},{1,0},{2,1},{3,2},{4,3},{5,4},{6,5},{7,6},{8,15},{9,8},{10,9... | collective-permute-start | bytes 884744 | tf_op jit(solution)/shard_map/ppermute | solution.py:30
  77.8 7.0 %collective-permute-done.11.refs_8_ = bf16[192,768]{1,0:T(8,128)(2,1)S(1)} collective-permute-done((bf16[192,768]{1,0:T(8,128)(2,1)S(1)}, bf16[192,768]{1,0:T(8,128)(2,1)S(1)}, u32[]{:S(2)}, u32[]{:S(2)}) %collective-permute-start.11) | collective-permute-done | bytes 294944 | tf_op jit(solution)/shard_map/ppermute | solution.py:30
  88.1 6.5 %collective-permute-done.12.refs_7_ = bf16[192,768]{1,0:T(8,128)(2,1)S(1)} collective-permute-done((bf16[192,768]{1,0:T(8,128)(2,1)S(1)}, bf16[192,768]{1,0:T(8,128)(2,1)S(1)}, u32[]{:S(2)}, u32[]{:S(2)}) %collective-permute-start.12) | collective-permute-done | bytes 294944 | tf_op jit(solution)/shard_map/ppermute | solution.py:30
  97.8 5.8 %collective-permute-done.13.refs_6_ = bf16[192,768]{1,0:T(8,128)(2,1)S(1)} collective-permute-done((bf16[192,768]{1,0:T(8,128)(2,1)S(1)}, bf16[192,768]{1,0:T(8,128)(2,1)S(1)}, u32[]{:S(2)}, u32[]{:S(2)}) %collective-permute-start.13) | collective-permute-done | bytes 294944 | tf_op jit(solution)/shard_map/ppermute | solution.py:30
  111.6 7.2 %project.5 = (bf16[4,256,384]{2,1,0:T(8,128)(2,1)}, bf16[4,256,384]{2,1,0:T(8,128)(2,1)}, bf16[4,256,384]{2,1,0:T(8,128)(2,1)}, bf16[4,256,768]{2,1,0:T(8,128)(2,1)}) custom-call(bf16[128,1536]{1,0:T(8,128)(2,1)} %copy-done.17, bf16[128,1536]{1,0:T(8,128)(2,1)} %copy-done.16, ...), custom_call_target="tpu_custom_call", output_to_operand_aliasing={{0}: (10, {}), {1}: (11, {}), {2}: (12, {}), {3}: (13, {})} | custom-call | tf_op jit(solution)/shard_map/project/pallas_call | solution.py:119
  122.4 4.8 %early_terms.3.ref.term_ref.own_ref = bf16[2,256,1536]{2,1,0:T(8,128)(2,1)S(1)} custom-call(bf16[4,256,384]{2,1,0:T(8,128)(2,1)S(1)} %copy-done.7, bf16[1024,384]{1,0:T(8,128)(2,1)S(1)} %bitcast.54, bf16[4,256,768]{2,1,0:T(8,128)(2,1)S(1)} %copy-done.1, bf16[192,1536]{1,0:T(8,128)(2,1)S(1)} %copy-done.12, bf16[768,1536]{1,0:T(8,128)(2,1)S(1)} %copy-done.5), custom_call_target="tpu_custom_call" | custom-call | tf_op jit(solution)/shard_map/early_terms/pallas_call | solution.py:207
  127.3 3.4 %collective-permute-start.18 = (bf16[64,1536]{1,0:T(8,128)(2,1)S(1)}, bf16[64,1536]{1,0:T(8,128)(2,1)S(1)}, u32[]{:S(2)}, u32[]{:S(2)}) collective-permute-start(bf16[64,1536]{1,0:T(8,128)(2,1)S(1)} %get-tuple-element.66), channel_id=1, source_target_pairs={{0,7},{1,0},{2,1},{3,2},{4,3},{5,4},{6,5},{7,6},{8,15},{9,8},{10,9... | collective-permute-start | bytes 589832 | tf_op jit(solution)/shard_map/ppermute | solution.py:30
  130.7 5.5 %collective-permute-done.17.ahead_ref = bf16[64,1536]{1,0:T(8,128)(2,1)S(1)} collective-permute-done((bf16[64,1536]{1,0:T(8,128)(2,1)S(1)}, bf16[64,1536]{1,0:T(8,128)(2,1)S(1)}, u32[]{:S(2)}, u32[]{:S(2)}) %collective-permute-start.17) | collective-permute-done | bytes 196640 | tf_op jit(solution)/shard_map/ppermute | solution.py:30
  142.3 6.7 %collective-permute-done.19.ahead_ref = bf16[128,1536]{1,0:T(8,128)(2,1)S(1)} collective-permute-done((bf16[128,1536]{1,0:T(8,128)(2,1)S(1)}, bf16[128,1536]{1,0:T(8,128)(2,1)S(1)}, u32[]{:S(2)}, u32[]{:S(2)}) %collective-permute-start.19) | collective-permute-done | bytes 393248 | tf_op jit(solution)/shard_map/ppermute | solution.py:30
  154.3 7.7 %cross_attention.1 = bf16[8,192,128]{2,1,0:T(8,128)(2,1)S(1)} custom-call(s32[40]{0:T(128)S(1)} %multiply_add_fusion.item_ref, s32[8]{0:T(128)S(1)} %dynamic-slice_reduce_fusion.count_ref, s32[1]{0:T(128)S(1)} %bitcast.58, bf16[4,256,384]{2,1,0:T(8,128)(2,1)S(1)} %copy-done.11, bf16[64,128,384]{2,1,0:T(8,128)(2,1)} %bitcast.14.received_ref), custom_call_target="tpu_custom_call" | custom-call | tf_op jit(solution)/shard_map/cross_attention/pallas_call | solution.py:303
  162.7 4.1 %all-to-all-start.1 = ((bf16[8,192,128]{2,1,0:T(8,128)(2,1)}), bf16[8,192,128]{2,1,0:T(8,128)(2,1)}, u32[]{:S(2)}, u32[]{:S(2)}) async-start(bf16[8,192,128]{2,1,0:T(8,128)(2,1)} %copy-done.14), calls=%async_computation.1 | async-start | bytes 786432 | tf_op jit(solution)/shard_map/all_to_all | solution.py:491
  176.8 9.7 %collective-permute-done.23.ahead_ref = bf16[128,1536]{1,0:T(8,128)(2,1)S(1)} collective-permute-done((bf16[128,1536]{1,0:T(8,128)(2,1)S(1)}, bf16[128,1536]{1,0:T(8,128)(2,1)S(1)}, u32[]{:S(2)}, u32[]{:S(2)}) %collective-permute-start.23) | collective-permute-done | bytes 393248 | tf_op jit(solution)/shard_map/ppermute | solution.py:30
  186.6 5.2 %finish.1 = bf16[128,1536]{1,0:T(8,128)(2,1)} custom-call(s32[2]{0:T(128)S(1)} %pad_add_fusion.1.place_ref, bf16[8,192,128]{2,1,0:T(8,128)(2,1)} %all-to-all-done.1.mix_ref, bf16[8,192,768]{2,1,0:T(8,128)(2,1)} %collect.1.mine_ref, bf16[8,192,768]{2,1,0:T(8,128)(2,1)} %collective-permute-done.16.other_ref, f32[128,1536]{1,0:T(8,128)S(1)} %earlier.1.base_ref), custom_call_target="tpu_custom_call" | custom-call | tf_op jit(solution)/shard_map/finish/pallas_call | solution.py:381
  (115 shorter events, 51.8 us)
Async XLA Ops:
  2.4 14.3 %collective-permute-start.4 = (bf16[128,1536]{1,0:T(8,128)(2,1)S(1)}, bf16[128,1536]{1,0:T(8,128)(2,1)S(1)}, u32[]{:S(2)}, u32[]{:S(2)}) collective-permute-start(bf16[128,1536]{1,0:T(8,128)(2,1)S(1)} %fusion.1.own_ref.refs_2_), channel_id=1, source_target_pairs={{0,7},{1,0},{2,1},{3,2},{4,3},{5,4},{6,5},{7,6},{8,15},{9,8},{10,9... | collective-permute-start | bytes 1179656 | tf_op jit(solution)/shard_map/ppermute | solution.py:30
  8.3 12.1 %collective-permute-start = (bf16[128,1536]{1,0:T(8,128)(2,1)S(1)}, bf16[128,1536]{1,0:T(8,128)(2,1)S(1)}, u32[]{:S(2)}, u32[]{:S(2)}) collective-permute-start(bf16[128,1536]{1,0:T(8,128)(2,1)S(1)} %fusion.1.own_ref.refs_2_), channel_id=1, source_target_pairs={{0,1},{1,2},{2,3},{3,4},{4,5},{5,6},{6,7},{7,0},{8,9},{9,10},{10,1... | collective-permute-start | bytes 1179656 | tf_op jit(solution)/shard_map/ppermute | solution.py:30
  16.7 11.2 %collective-permute-start.5 = (bf16[128,1536]{1,0:T(8,128)(2,1)S(1)}, bf16[128,1536]{1,0:T(8,128)(2,1)S(1)}, u32[]{:S(2)}, u32[]{:S(2)}) collective-permute-start(bf16[128,1536]{1,0:T(8,128)(2,1)S(1)} %collective-permute-done.4.refs_1_), channel_id=1, source_target_pairs={{0,7},{1,0},{2,1},{3,2},{4,3},{5,4},{6,5},{7,6},{8,15},{9,8},{10,9... | collective-permute-start | bytes 1179656 | tf_op jit(solution)/shard_map/ppermute | solution.py:30
  20.4 11.2 %collective-permute-start.1 = (bf16[128,1536]{1,0:T(8,128)(2,1)S(1)}, bf16[128,1536]{1,0:T(8,128)(2,1)S(1)}, u32[]{:S(2)}, u32[]{:S(2)}) collective-permute-start(bf16[128,1536]{1,0:T(8,128)(2,1)S(1)} %collective-permute-done.refs_0_), channel_id=1, source_target_pairs={{0,1},{1,2},{2,3},{3,4},{4,5},{5,6},{6,7},{7,0},{8,9},{9,10},{10,1... | collective-permute-start | bytes 1179656 | tf_op jit(solution)/shard_map/ppermute | solution.py:30
  27.9 10.4 %collective-permute-start.6 = (bf16[128,1536]{1,0:T(8,128)(2,1)S(1)}, bf16[128,1536]{1,0:T(8,128)(2,1)S(1)}, u32[]{:S(2)}, u32[]{:S(2)}) collective-permute-start(bf16[128,1536]{1,0:T(8,128)(2,1)S(1)} %collective-permute-done.5.refs_1_), channel_id=1, source_target_pairs={{0,7},{1,0},{2,1},{3,2},{4,3},{5,4},{6,5},{7,6},{8,15},{9,8},{10,9... | collective-permute-start | bytes 1179656 | tf_op jit(solution)/shard_map/ppermute | solution.py:30
  31.6 10.4 %collective-permute-start.2 = (bf16[128,1536]{1,0:T(8,128)(2,1)S(1)}, bf16[128,1536]{1,0:T(8,128)(2,1)S(1)}, u32[]{:S(2)}, u32[]{:S(2)}) collective-permute-start(bf16[128,1536]{1,0:T(8,128)(2,1)S(1)} %collective-permute-done.1.refs_0_), channel_id=1, source_target_pairs={{0,1},{1,2},{2,3},{3,4},{4,5},{5,6},{6,7},{7,0},{8,9},{9,10},{10,1... | collective-permute-start | bytes 1179656 | tf_op jit(solution)/shard_map/ppermute | solution.py:30
  38.3 19.9 %collective-permute-start.7 = (bf16[64,1536]{1,0:T(8,128)(2,1)S(1)}, bf16[64,1536]{1,0:T(8,128)(2,1)S(1)}, u32[]{:S(2)}, u32[]{:S(2)}) collective-permute-start(bf16[64,1536]{1,0:T(8,128)(2,1)S(1)} %slice.21), channel_id=1, source_target_pairs={{0,7},{1,0},{2,1},{3,2},{4,3},{5,4},{6,5},{7,6},{8,15},{9,8},{10,9... | collective-permute-start | bytes 589832 | tf_op jit(solution)/shard_map/ppermute | solution.py:30
  42.8 15.5 %collective-permute-start.3 = (bf16[64,1536]{1,0:T(8,128)(2,1)}, bf16[64,1536]{1,0:T(8,128)(2,1)S(1)}, u32[]{:S(2)}, u32[]{:S(2)}) collective-permute-start(bf16[64,1536]{1,0:T(8,128)(2,1)} %slice.20), channel_id=1, source_target_pairs={{0,1},{1,2},{2,3},{3,4},{4,5},{5,6},{6,7},{7,0},{8,9},{9,10},{10,1... | collective-permute-start | bytes 589832 | tf_op jit(solution)/shard_map/ppermute | solution.py:30
  66.7 86.5 %all-to-all-start = ((bf16[32,2,128,384]{3,2,1,0:T(8,128)(2,1)}), bf16[32,2,128,384]{3,2,1,0:T(8,128)(2,1)}, u32[]{:S(2)}, u32[]{:S(2)}) async-start(bf16[32,2,128,384]{3,2,1,0:T(8,128)(2,1)} %pack_items.1), calls=%async_computation | async-start | bytes 12582912 | tf_op jit(solution)/shard_map/all_to_all | solution.py:467
  74.2 10.6 %collective-permute-start.11 = (bf16[192,768]{1,0:T(8,128)(2,1)S(1)}, bf16[192,768]{1,0:T(8,128)(2,1)S(1)}, u32[]{:S(2)}, u32[]{:S(2)}) collective-permute-start(bf16[192,768]{1,0:T(8,128)(2,1)S(1)} %constant_dynamic-slice_fusion.refs_0_), channel_id=1, source_target_pairs={{0,1},{1,2},{2,3},{3,4},{4,5},{5,6},{6,7},{7,0},{8,9},{9,10},{10,1... | collective-permute-start | bytes 884744 | tf_op jit(solution)/shard_map/ppermute | solution.py:30
  74.3 10.5 %collective-permute-start.8 = (bf16[192,768]{1,0:T(8,128)(2,1)S(1)}, bf16[192,768]{1,0:T(8,128)(2,1)S(1)}, u32[]{:S(2)}, u32[]{:S(2)}) collective-permute-start(bf16[192,768]{1,0:T(8,128)(2,1)S(1)} %constant_dynamic-slice_fusion.refs_0_), channel_id=1, source_target_pairs={{0,7},{1,0},{2,1},{3,2},{4,3},{5,4},{6,5},{7,6},{8,15},{9,8},{10,9... | collective-permute-start | bytes 884744 | tf_op jit(solution)/shard_map/ppermute | solution.py:30
  84.8 9.8 %collective-permute-start.12 = (bf16[192,768]{1,0:T(8,128)(2,1)S(1)}, bf16[192,768]{1,0:T(8,128)(2,1)S(1)}, u32[]{:S(2)}, u32[]{:S(2)}) collective-permute-start(bf16[192,768]{1,0:T(8,128)(2,1)S(1)} %collective-permute-done.11.refs_8_), channel_id=1, source_target_pairs={{0,1},{1,2},{2,3},{3,4},{4,5},{5,6},{6,7},{7,0},{8,9},{9,10},{10,1... | collective-permute-start | bytes 884744 | tf_op jit(solution)/shard_map/ppermute | solution.py:30
  84.8 9.8 %collective-permute-start.9 = (bf16[192,768]{1,0:T(8,128)(2,1)S(1)}, bf16[192,768]{1,0:T(8,128)(2,1)S(1)}, u32[]{:S(2)}, u32[]{:S(2)}) collective-permute-start(bf16[192,768]{1,0:T(8,128)(2,1)S(1)} %collective-permute-done.8.refs_1_), channel_id=1, source_target_pairs={{0,7},{1,0},{2,1},{3,2},{4,3},{5,4},{6,5},{7,6},{8,15},{9,8},{10,9... | collective-permute-start | bytes 884744 | tf_op jit(solution)/shard_map/ppermute | solution.py:30
  94.6 9.0 %collective-permute-start.13 = (bf16[192,768]{1,0:T(8,128)(2,1)S(1)}, bf16[192,768]{1,0:T(8,128)(2,1)S(1)}, u32[]{:S(2)}, u32[]{:S(2)}) collective-permute-start(bf16[192,768]{1,0:T(8,128)(2,1)S(1)} %collective-permute-done.12.refs_7_), channel_id=1, source_target_pairs={{0,1},{1,2},{2,3},{3,4},{4,5},{5,6},{6,7},{7,0},{8,9},{9,10},{10,1... | collective-permute-start | bytes 884744 | tf_op jit(solution)/shard_map/ppermute | solution.py:30
  94.6 9.1 %collective-permute-start.10 = (bf16[192,768]{1,0:T(8,128)(2,1)S(1)}, bf16[192,768]{1,0:T(8,128)(2,1)S(1)}, u32[]{:S(2)}, u32[]{:S(2)}) collective-permute-start(bf16[192,768]{1,0:T(8,128)(2,1)S(1)} %collective-permute-done.9.refs_2_), channel_id=1, source_target_pairs={{0,7},{1,0},{2,1},{3,2},{4,3},{5,4},{6,5},{7,6},{8,15},{9,8},{10,9... | collective-permute-start | bytes 884744 | tf_op jit(solution)/shard_map/ppermute | solution.py:30
  111.6 75.0 %collective-permute-start.16 = (bf16[8,192,768]{2,1,0:T(8,128)(2,1)}, bf16[8,192,768]{2,1,0:T(8,128)(2,1)}, u32[]{:S(2)}, u32[]{:S(2)}) collective-permute-start(bf16[8,192,768]{2,1,0:T(8,128)(2,1)} %collect.1.mine_ref), channel_id=1, source_target_pairs={{0,8},{8,0},{16,24},{24,16},{32,40},{40,32},{48,56},{56,48},{64,72... | collective-permute-start | bytes 7077896 | tf_op jit(solution)/shard_map/ppermute | solution.py:478
  127.3 9.0 %collective-permute-start.17 = (bf16[64,1536]{1,0:T(8,128)(2,1)S(1)}, bf16[64,1536]{1,0:T(8,128)(2,1)S(1)}, u32[]{:S(2)}, u32[]{:S(2)}) collective-permute-start(bf16[64,1536]{1,0:T(8,128)(2,1)S(1)} %get-tuple-element.65), channel_id=1, source_target_pairs={{0,1},{1,2},{2,3},{3,4},{4,5},{5,6},{6,7},{7,0},{8,9},{9,10},{10,1... | collective-permute-start | bytes 589832 | tf_op jit(solution)/shard_map/ppermute | solution.py:30
  136.3 12.6 %collective-permute-start.19 = (bf16[128,1536]{1,0:T(8,128)(2,1)S(1)}, bf16[128,1536]{1,0:T(8,128)(2,1)S(1)}, u32[]{:S(2)}, u32[]{:S(2)}) collective-permute-start(bf16[128,1536]{1,0:T(8,128)(2,1)S(1)} %get-tuple-element.67), channel_id=1, source_target_pairs={{0,1},{1,2},{2,3},{3,4},{4,5},{5,6},{6,7},{7,0},{8,9},{9,10},{10,1... | collective-permute-start | bytes 1179656 | tf_op jit(solution)/shard_map/ppermute | solution.py:30
  136.8 12.1 %collective-permute-start.20 = (bf16[128,1536]{1,0:T(8,128)(2,1)S(1)}, bf16[128,1536]{1,0:T(8,128)(2,1)S(1)}, u32[]{:S(2)}, u32[]{:S(2)}) collective-permute-start(bf16[128,1536]{1,0:T(8,128)(2,1)S(1)} %get-tuple-element.68), channel_id=1, source_target_pairs={{0,7},{1,0},{2,1},{3,2},{4,3},{5,4},{6,5},{7,6},{8,15},{9,8},{10,9... | collective-permute-start | bytes 1179656 | tf_op jit(solution)/shard_map/ppermute | solution.py:30
  149.9 22.1 %collective-permute-start.21 = (bf16[128,1536]{1,0:T(8,128)(2,1)}, bf16[128,1536]{1,0:T(8,128)(2,1)}, u32[]{:S(2)}, u32[]{:S(2)}) collective-permute-start(bf16[128,1536]{1,0:T(8,128)(2,1)} %get-tuple-element.69), channel_id=1, source_target_pairs={{0,1},{1,2},{2,3},{3,4},{4,5},{5,6},{6,7},{7,0},{8,9},{9,10},{10,1... | collective-permute-start | bytes 1179656 | tf_op jit(solution)/shard_map/ppermute | solution.py:30
  149.9 22.1 %collective-permute-start.22 = (bf16[128,1536]{1,0:T(8,128)(2,1)}, bf16[128,1536]{1,0:T(8,128)(2,1)}, u32[]{:S(2)}, u32[]{:S(2)}) collective-permute-start(bf16[128,1536]{1,0:T(8,128)(2,1)} %get-tuple-element.70), channel_id=1, source_target_pairs={{0,7},{1,0},{2,1},{3,2},{4,3},{5,4},{6,5},{7,6},{8,15},{9,8},{10,9... | collective-permute-start | bytes 1179656 | tf_op jit(solution)/shard_map/ppermute | solution.py:30
  162.7 23.9 %all-to-all-start.1 = ((bf16[8,192,128]{2,1,0:T(8,128)(2,1)}), bf16[8,192,128]{2,1,0:T(8,128)(2,1)}, u32[]{:S(2)}, u32[]{:S(2)}) async-start(bf16[8,192,128]{2,1,0:T(8,128)(2,1)} %copy-done.14), calls=%async_computation.1 | async-start | bytes 786432 | tf_op jit(solution)/shard_map/all_to_all | solution.py:491
  173.4 13.0 %collective-permute-start.23 = (bf16[128,1536]{1,0:T(8,128)(2,1)S(1)}, bf16[128,1536]{1,0:T(8,128)(2,1)S(1)}, u32[]{:S(2)}, u32[]{:S(2)}) collective-permute-start(bf16[128,1536]{1,0:T(8,128)(2,1)S(1)} %get-tuple-element.71), channel_id=1, source_target_pairs={{0,1},{1,2},{2,3},{3,4},{4,5},{5,6},{6,7},{7,0},{8,9},{9,10},{10,1... | collective-permute-start | bytes 1179656 | tf_op jit(solution)/shard_map/ppermute | solution.py:30
  175.4 11.0 %collective-permute-start.24 = (bf16[128,1536]{1,0:T(8,128)(2,1)S(1)}, bf16[128,1536]{1,0:T(8,128)(2,1)S(1)}, u32[]{:S(2)}, u32[]{:S(2)}) collective-permute-start(bf16[128,1536]{1,0:T(8,128)(2,1)S(1)} %get-tuple-element.72), channel_id=1, source_target_pairs={{0,7},{1,0},{2,1},{3,2},{4,3},{5,4},{6,5},{7,6},{8,15},{9,8},{10,9... | collective-permute-start | bytes 1179656 | tf_op jit(solution)/shard_map/ppermute | solution.py:30
  (27 other events, 262.4 us)
